TPU v7x, 32 devices: a whole 2x2x4 slice. The times are simulated.
32 devices in a mesh: dp: 8 (over y, x, core), fsdp: 4 (over z).
Axes of the slice: x: 2, y: 2, z: 4, core: 2. Of those that a mesh axis runs over, the one named last changes fastest.
Arguments:
- img_emb: bfloat16 [1024, 1024], P(('dp', 'fsdp')), may hold values from -0.25 to 0.25
- txt_emb: bfloat16 [1024, 1024], P(('dp', 'fsdp')), may hold values from -0.25 to 0.25
- img_ids: int32 [1024], P(('dp', 'fsdp')), may hold values from 0 to 1023
- txt_ids: int32 [1024], P(('dp', 'fsdp')), may hold values from 0 to 1023
- temp_log: float32 [1], replicated, may hold values from 1.5 to 2.5
- logit_bias: float32 [1], replicated, may hold values from -6 to -2
- block_in: bfloat16 [2048, 3072], P(('dp', 'fsdp')), may hold values from -6 to 6
- dw_kernel: float32 [49, 3072], replicated, may hold values from -0.875 to 0.875
- ln_gain: float32 [3072], replicated, may hold values from 0.5 to 1.5
- ln_bias: float32 [3072], replicated, may hold values from -3 to 3
- w_up: bfloat16 [3072, 6144], P(None, 'fsdp'), may hold values from -0.109375 to 0.109375
- w_down: bfloat16 [6144, 3072], P('fsdp'), may hold values from -0.078125 to 0.078125
- layer_scale: float32 [3072], replicated, may hold values from 0.1 to 1
- head_gain: float32 [3072], replicated, may hold values from 0.5 to 1.5
- head_bias: float32 [3072], replicated, may hold values from -3 to 3
- w_proj: bfloat16 [3072, 1024], replicated, may hold values from -0.109375 to 0.109375
Outputs:
- img_grad: float32 [1024, 1024], P(('dp', 'fsdp'))
- txt_grad: float32 [1024, 1024], P(('dp', 'fsdp'))
- w_up_grad: float32 [3072, 6144], P('dp', 'fsdp')
- w_down_grad: float32 [6144, 3072], P('fsdp', 'dp')
All inputs are finite; a program needn't handle non-finite values.
Results may differ from a plain program's by a relative error of at most 0.02.
Values may be sent and summed in bfloat16 or wider, within the bound.
A program may use at most 128 MiB of HBM per device.

v0:
```python
import jax
import jax.numpy as jnp
from jax import lax
from jax.sharding import PartitionSpec as P

KERNEL = 7
SIDE = 8


def unit_rows(matrix):
    values = matrix.astype(jnp.float32)
    length = jnp.sqrt(jnp.sum(values * values, axis=1, keepdims=True) + 1e-06)
    return (values / length, length)


def back_unit(gradient, unit_part, length):
    inner_prod = jnp.sum(unit_part * gradient, axis=1, keepdims=True)
    return (gradient - unit_part * inner_prod) / length


def pair_tile(images, image_ids, text_rows, text_ids, temper, offset):
    scores = jnp.dot(images, text_rows.T, preferred_element_type=jnp.float32)
    logits = temper * scores + offset
    labels = jnp.where(image_ids[:, None] == text_ids[None, :], 1.0, -1.0)
    weights = (temper * -labels * jax.nn.sigmoid(-labels * logits)).astype(jnp.bfloat16)
    image_part = jnp.dot(weights, text_rows, preferred_element_type=jnp.float32)
    text_part = jnp.dot(weights.T, images, preferred_element_type=jnp.float32)
    return (image_part, text_part)


def depthwise(pictures, kernel):
    reach = KERNEL // 2
    padded = jnp.pad(pictures, ((0, 0), (reach, reach), (reach, reach), (0, 0)))
    summed = jnp.zeros_like(pictures)
    for above in range(KERNEL):
        for across in range(KERNEL):
            summed = (
                summed
                + kernel[above * KERNEL + across]
                * padded[:, above : above + SIDE, across : across + SIDE, :]
            )
    return summed


def layer_norm(values, gain_vec, bias_vec):
    centre = jnp.mean(values, axis=-1, keepdims=True)
    centred = values - centre
    inverse = 1.0 / jnp.sqrt(jnp.mean(centred * centred, axis=-1, keepdims=True) + 1e-06)
    normal = centred * inverse
    return (normal * gain_vec + bias_vec, normal, inverse)


def head_back(patch_means, block_mean, image_sum, layer_scale, head_gain, head_bias, w_proj):
    pooled = patch_means.astype(jnp.float32) + layer_scale * block_mean
    head_out, head_norm, inverse = layer_norm(pooled, head_gain, head_bias)
    embed = jnp.dot(head_out.astype(jnp.bfloat16), w_proj, preferred_element_type=jnp.float32)
    embed_unit, embed_len = unit_rows(embed)
    embed_grad = back_unit(image_sum, embed_unit, embed_len).astype(jnp.bfloat16)
    head_grad = jnp.dot(embed_grad, w_proj.T, preferred_element_type=jnp.float32)
    norm_grad = head_grad * head_gain
    pool_grad = inverse * (
        norm_grad
        - jnp.mean(norm_grad, axis=1, keepdims=True)
        - head_norm * jnp.mean(norm_grad * head_norm, axis=1, keepdims=True)
    )
    return (layer_scale * pool_grad / (SIDE * SIDE)).astype(jnp.bfloat16)


def on_device(
    img_emb,
    txt_emb,
    img_ids,
    txt_ids,
    temp_log,
    logit_bias,
    block_in,
    dw_kernel,
    ln_gain,
    ln_bias,
    w_up,
    w_down,
    layer_scale,
    head_gain,
    head_bias,
    w_proj,
):
    channels = block_in.shape[1]
    hid_width = w_up.shape[1]
    temper = jnp.exp(temp_log[0])
    offset = logit_bias[0]
    img_unit, img_len = unit_rows(img_emb)
    txt_unit, txt_len = unit_rows(txt_emb)
    img_b = img_unit.astype(jnp.bfloat16)
    txt_b = txt_unit.astype(jnp.bfloat16)
    pictures = block_in.astype(jnp.float32).reshape(1, SIDE, SIDE, channels)
    mixed_rows = depthwise(pictures, dw_kernel).reshape(SIDE * SIDE, channels)
    normed = layer_norm(mixed_rows, ln_gain, ln_bias)[0].astype(jnp.bfloat16)
    patch_means = jnp.mean(pictures, axis=(1, 2)).astype(jnp.bfloat16)
    group_img, group_ids, group_normed = (
        lax.all_gather(img_b, "fsdp", axis=0, tiled=True),
        lax.all_gather(img_ids, "fsdp", axis=0, tiled=True),
        lax.all_gather(normed, "fsdp", axis=0, tiled=True),
    )
    image_count = group_normed.shape[0] // (SIDE * SIDE)
    image_part, text_part = pair_tile(
        group_img,
        group_ids,
        lax.all_gather(txt_b, "dp", axis=0, tiled=True),
        lax.all_gather(txt_ids, "dp", axis=0, tiled=True),
        temper,
        offset,
    )
    image_acc = image_part
    image_acc = lax.optimization_barrier(image_acc.astype(jnp.bfloat16)).astype(jnp.float32)
    hidden = jnp.dot(group_normed, w_up, preferred_element_type=jnp.float32)
    active = jax.nn.gelu(hidden).astype(jnp.bfloat16)
    active_total = jnp.sum(
        active.astype(jnp.float32).reshape(image_count, SIDE * SIDE, hid_width), axis=1
    )
    down_wide = w_down.astype(jnp.float32)
    partial_mean = jnp.dot(active_total / (SIDE * SIDE), down_wide, precision=lax.Precision.HIGHEST)
    image_sum, block_mean = (
        lax.psum_scatter(
            image_acc.astype(jnp.bfloat16), "fsdp", scatter_dimension=0, tiled=True
        ).astype(jnp.float32),
        lax.psum_scatter(
            partial_mean.astype(jnp.bfloat16), "fsdp", scatter_dimension=0, tiled=True
        ).astype(jnp.float32),
    )
    grad_row = head_back(
        patch_means, block_mean, image_sum[:1], layer_scale, head_gain, head_bias, w_proj
    )
    group_grad = lax.all_gather(grad_row, "fsdp", axis=0, tiled=True)
    row_down = jnp.dot(group_grad, w_down.T, preferred_element_type=jnp.float32)
    down_grad = jnp.broadcast_to(
        row_down[:, None, :], (image_count, SIDE * SIDE, hid_width)
    ).reshape(-1, hid_width)
    _, pullback = jax.vjp(jax.nn.gelu, hidden)
    hid_grad = pullback(down_grad)[0].astype(jnp.bfloat16)
    down_part = jnp.dot(
        active_total.T, group_grad.astype(jnp.float32), precision=lax.Precision.HIGHEST
    )
    up_part = jnp.dot(group_normed.T, hid_grad, preferred_element_type=jnp.float32)
    w_up_grad, w_down_grad, text_sum = (
        lax.psum_scatter(
            up_part.astype(jnp.bfloat16), "dp", scatter_dimension=0, tiled=True
        ).astype(jnp.float32),
        lax.psum_scatter(
            down_part.astype(jnp.bfloat16), "dp", scatter_dimension=1, tiled=True
        ).astype(jnp.float32),
        lax.psum_scatter(
            text_part.astype(jnp.bfloat16), "dp", scatter_dimension=0, tiled=True
        ).astype(jnp.float32),
    )
    img_grad = back_unit(image_sum, img_unit, img_len)
    txt_grad = back_unit(text_sum, txt_unit, txt_len)
    return (img_grad, txt_grad, w_up_grad, w_down_grad)


def solution(mesh):
    in_specs = (
        P(("dp", "fsdp"), None),
        P(("dp", "fsdp"), None),
        P(("dp", "fsdp")),
        P(("dp", "fsdp")),
        P(),
        P(),
        P(("dp", "fsdp"), None),
        P(),
        P(),
        P(),
        P(None, "fsdp"),
        P("fsdp", None),
        P(),
        P(),
        P(),
        P(),
    )
    out_specs = (P(("dp", "fsdp"), None), P(("dp", "fsdp"), None), P("dp", "fsdp"), P("fsdp", "dp"))
    return jax.shard_map(
        on_device, mesh=mesh, in_specs=in_specs, out_specs=out_specs, check_vma=False
    )
```

profile of v0, /device:TPU:0, one launch (start us, length us, event | category | flops | bytes accessed | tf_op | source)
XLA Modules:
  0.0 363.6 jit_solution(8530367770583388540)
XLA Ops:
  8.5 1.2 dynamic-slice.1
  10.4 1.4 fusion.155
  12.5 1.0 fusion.118
  13.5 1.0 fusion.119
  15.3 9.9 %all-reduce.1 = s32[128]{0:T(128)S(1)} all-reduce(s32[128]{0:T(128)S(1)} %dynamic-update-slice), channel_id=1, replica_groups=mesh['dp'=8,'fsdp'=4] {'fsdp'}, use_global_device_ids=true, to_apply=%add.1 | all-reduce | flops 128 | bytes 1024
  26.1 8.0 %all-reduce.2 = s32[256]{0:T(256)S(1)} all-reduce(s32[256]{0:T(256)S(1)} %dynamic-update-slice.1), channel_id=1, replica_groups=mesh['dp'=8,'fsdp'=4] {'dp'}, use_global_device_ids=true, to_apply=%add.2 | all-reduce | flops 256 | bytes 2048
  35.9 14.2 %all_gather.20 = bf16[128,1024]{1,0:T(8,128)(2,1)S(1)} all-gather(bf16[32,1024]{1,0:T(8,128)(2,1)S(1)} %fusion.145), channel_id=1, replica_groups=mesh['dp'=8,'fsdp'=4] {'fsdp'}, dimensions={0}, use_global_device_ids=true | all-gather | bytes 327680 | tf_op jit(solution)/shard_map/all_gather | solution.py:100
  50.2 9.0 %all_gather.21 = bf16[256,1024]{1,0:T(8,128)(2,1)S(1)} all-gather(bf16[32,1024]{1,0:T(8,128)(2,1)S(1)} %fusion.146), channel_id=1, replica_groups=mesh['dp'=8,'fsdp'=4] {'dp'}, dimensions={0}, use_global_device_ids=true | all-gather | bytes 589824 | tf_op jit(solution)/shard_map/all_gather | solution.py:108
  61.1 5.5 %fusion.150 = (f32[8,8]{1,0:T(8,128)S(1)}, f32[1,8,8,3072]{3,2,1,0:T(8,128)S(1)}) fusion(f32[3072]{0:T(1024)S(1)} %bitcast.138, f32[3072]{0:T(1024)S(1)} %bitcast.139, f32[3072]{0:T(1024)S(1)} %bitcast.142, f32[3072]{0:T(1024)S(1)} %bitcast.143, f32[3072]{0:T(1024)S(1)} %bitcast.144, f32[3072]{0:T(1024)S(1)} %bitcast.145, f32[3072]{0:T(1024)S(1)} %bitcast.146, ...), kind=kLoop, calls=%fused_computation.236 | loop fusion | flops 19267520 | bytes 2175232 | tf_op jit(solution)/shard_map/reduce_sum | solution.py:46
  67.0 0.9 fusion.117
  68.0 1.1 convolution_convert_fusion.3
  69.3 10.2 %reduce-scatter.7.cloned.1.call-done = bf16[32,1024]{1,0:T(8,128)(2,1)} async-done(((bf16[128,1024]{1,0:T(8,128)(2,1)}), bf16[32,1024]{1,0:T(8,128)(2,1)}) %reduce-scatter.7.cloned.1.call-update) | async-done | bytes 65552 | tf_op jit(solution)/shard_map/reduce_scatter | solution.py:123
  80.4 36.6 %all-gather.3.cloned.1.call-done = bf16[256,3072]{1,0:T(8,128)(2,1)} async-done(((bf16[64,3072]{1,0:T(8,128)(2,1)}), bf16[256,3072]{1,0:T(8,128)(2,1)}) %all-gather.3.cloned.1.call-update) | async-done | bytes 1572880 | tf_op jit(solution)/shard_map/all_gather | solution.py:102
  117.0 5.9 %convert_reduce_fusion = (f32[4,1536]{1,0:T(4,128)S(1)}, f32[256,1536]{1,0:T(8,128)S(1)}) fusion(bf16[256,3072]{1,0:T(8,128)(2,1)} %all-gather.3.cloned.1.call-done, bf16[3072,1536]{1,0:T(8,128)(2,1)} %param.26), kind=kOutput, calls=%fused_computation.65 | convolution fusion | flops 2420238336 | bytes 12607488 | tf_op jit(solution)/shard_map/dot_general | solution.py:115
  122.9 6.3 %convolution_convert_fusion.2 = bf16[4,3072]{1,0:T(4,128)(2,1)S(1)} fusion(bf16[1536,3072]{1,0:T(8,128)(2,1)} %param.27, f32[4,1536]{1,0:T(4,128)S(1)} %get-tuple-element.61), kind=kOutput, calls=%fused_computation.50 | convolution fusion | flops 226510848 | bytes 9486336 | tf_op jit(solution)/shard_map/dot_general | solution.py:121
  129.2 16.9 %all-reduce.3 = bf16[4,3072]{1,0:T(4,128)(2,1)S(1)} all-reduce(bf16[4,3072]{1,0:T(4,128)(2,1)S(1)} %convolution_convert_fusion.2), channel_id=4, replica_groups=mesh['dp'=8,'fsdp'=4] {'fsdp'}, use_global_device_ids=true, to_apply=%region_10.11.clone | all-reduce | flops 12288 | bytes 49152
  146.1 1.3 fusion.148
  149.4 3.7 %fusion.126 = f32[1,1024]{1,0:T(1,128)S(1)} fusion(bf16[3072,1024]{1,0:T(8,128)(2,1)} %param.31, f32[1,3072]{1,0:T(1,128)S(1)} %bitcast.186, f32[1,3072]{1,0:T(1,128)S(1)} %bitcast.183, f32[1,3072]{1,0:T(1,128)S(1)} %get-tuple-element.7, f32[]{:T(128)S(6)} %sqrt.32, f32[]{:T(128)S(6)} %div.98), kind=kOutput, calls=%fused_computation.198 | convolution fusion | flops 6306816 | bytes 6332424 | tf_op jit(solution)/shard_map/dot_general | solution.py:56
  155.7 4.5 %fusion.137 = f32[1,3072]{1,0:T(1,128)S(1)} fusion(bf16[3072,1024]{1,0:T(8,128)(2,1)} %param.31, f32[1,1024]{1,0:T(1,128)S(1)} %bitcast.184, f32[32,1024]{1,0:T(8,128)S(1)} %convert_element_type.105, f32[]{:T(128)S(6)} %sqrt.33), kind=kOutput, calls=%fused_computation.216 | convolution fusion | flops 6294528 | bytes 6311940 | tf_op jit(solution)/shard_map/dot_general | solution.py:59
  162.8 13.3 %all-gather = bf16[4,1,3072]{2,1,0:T(2,128)(2,1)S(1)} all-gather(bf16[1,1,3072]{2,1,0:T(2,128)(2,1)S(1)} %convert_bitcast_fusion.1), channel_id=1, replica_groups=mesh['dp'=8,'fsdp'=4] {'fsdp'}, dimensions={0}, use_global_device_ids=true | all-gather | bytes 30720 | tf_op jit(solution)/shard_map/all_gather | solution.py:133
  176.1 9.7 %convolution_convert_fusion = bf16[1536,3072]{1,0:T(8,128)(2,1)} fusion(f32[4,1536]{1,0:T(4,128)S(1)} %get-tuple-element.61, bf16[4,1,3072]{2,1,0:T(2,128)(2,1)S(1)} %all-gather), kind=kOutput, calls=%fused_computation.48 | convolution fusion | flops 231211008 | bytes 9486336 | tf_op jit(solution)/shard_map/dot_general | solution.py:140
  185.8 12.7 %copy.20 = bf16[1536,3072]{0,1:T(8,128)(2,1)} copy(bf16[1536,3072]{1,0:T(8,128)(2,1)} %convolution_convert_fusion) | data formatting | bytes 18874368
  198.6 6.2 %fusion.123 = f32[4,1536]{1,0:T(4,128)S(1)} fusion(bf16[1536,3072]{1,0:T(8,128)(2,1)} %param.27, bf16[4,1,3072]{2,1,0:T(2,128)(2,1)S(1)} %all-gather), kind=kOutput, calls=%fused_computation.195 | convolution fusion | flops 37748736 | bytes 9486336 | tf_op jit(solution)/shard_map/dot_general | solution.py:134
  204.8 1.1 fusion.6
  206.6 6.4 %convolution_convert_fusion.1 = bf16[3072,1536]{1,0:T(8,128)(2,1)} fusion(bf16[256,3072]{1,0:T(8,128)(2,1)S(1)} %copy-done, bf16[256,1536]{1,0:T(8,128)(2,1)S(1)} %fusion.6), kind=kOutput, calls=%fused_computation.49 | convolution fusion | flops 2420637696 | bytes 11796480 | tf_op jit(solution)/shard_map/dot_general | solution.py:143
  214.8 1.0 fusion.120
  215.8 1.6 fusion.121
  217.4 56.5 %reduce-scatter.13.cloned.1.call-done = bf16[384,1536]{1,0:T(8,128)(2,1)} async-done(((bf16[3072,1536]{1,0:T(8,128)(2,1)}), bf16[384,1536]{1,0:T(8,128)(2,1)}) %reduce-scatter.13.cloned.1.call-update) | async-done | bytes 1179664
  273.9 1.7 copy.21
  275.6 1.6 convert_element_type.123
  277.2 76.9 %reduce-scatter.11.cloned.1.call-done = bf16[384,1536]{1,0:T(8,128)(2,1)} async-done(((bf16[3072,1536]{1,0:T(8,128)(2,1)}), bf16[384,1536]{1,0:T(8,128)(2,1)}) %reduce-scatter.11.cloned.1.call-update) | async-done | bytes 1179664 | tf_op jit(solution)/shard_map/reduce_scatter | solution.py:145
  354.1 3.0 convert_element_type.121
  (66 shorter events, 13.3 us)
Async XLA Ops:
  7.2 72.4 %reduce-scatter.7.cloned.1.call-start = ((), (), s32[]{:S(2)}) async-start(), calls=%async_computation.4 | async-start | bytes 327680 | tf_op jit(solution)/shard_map/reduce_scatter | solution.py:123
  50.2 10.3 %copy-start.5 = (f32[49,3072]{1,0:T(8,128)S(1)}, f32[49,3072]{1,0:T(8,128)}, u32[]{:S(2)}) copy-start(f32[49,3072]{1,0:T(8,128)} %param.23) | copy-start | bytes 1806340
  59.2 1.8 copy-start.1
  60.5 56.5 %all-gather.3.cloned.1.call-start = ((), (), s32[]{:S(2)}) async-start(), calls=%async_computation.6 | async-start | bytes 1966080 | tf_op jit(solution)/shard_map/all_gather | solution.py:102
  61.0 6.0 %copy-start.8 = (f32[3072]{0:T(1024)S(1)}, f32[3072]{0:T(1024)}, u32[]{:S(2)}) copy-start(f32[3072]{0:T(1024)} %param.25) | copy-start | bytes 36868
  61.1 5.9 %copy-start.9 = (f32[3072]{0:T(1024)S(1)}, f32[3072]{0:T(1024)}, u32[]{:S(2)}) copy-start(f32[3072]{0:T(1024)} %param.24) | copy-start | bytes 36868
  68.0 146.8 %reduce-scatter.9.cloned.1.call-start = ((), (), s32[]{:S(2)}) async-start(), calls=%async_computation.5 | async-start | bytes 589824 | tf_op jit(solution)/shard_map/reduce_scatter | solution.py:151
  69.2 204.7 %reduce-scatter.13.cloned.1.call-start = ((), (), s32[]{:S(2)}) async-start(), calls=%async_computation.8 | async-start | bytes 10616832
  122.9 23.2 %copy-start.6 = (f32[3072]{0:T(1024)S(1)}, f32[3072]{0:T(1024)}, u32[]{:S(2)}) copy-start(f32[3072]{0:T(1024)} %param.28) | copy-start | bytes 36868
  122.9 26.5 %copy-start.7 = (f32[3072]{0:T(1024)S(1)}, f32[3072]{0:T(1024)}, u32[]{:S(2)}) copy-start(f32[3072]{0:T(1024)} %param.29) | copy-start | bytes 36868
  122.9 26.5 %copy-start.10 = (f32[3072]{0:T(1024)S(1)}, f32[3072]{0:T(1024)}, u32[]{:S(2)}) copy-start(f32[3072]{0:T(1024)} %param.30) | copy-start | bytes 36868
  198.5 155.6 %reduce-scatter.11.cloned.1.call-start = ((), (), s32[]{:S(2)}) async-start(), calls=%async_computation.7 | async-start | bytes 10616832 | tf_op jit(solution)/shard_map/reduce_scatter | solution.py:145
  204.8 1.8 copy-start
  212.9 0.8 copy-start.2
  212.9 0.9 copy-start.4
  212.9 1.8 copy-start.3
Sparse Core Ops, SparseCore 0:
  60.6 18.9 reduce-scatter.6
  81.7 35.2 all-gather.2
  120.7 32.9 reduce-scatter.8
  198.6 75.2 reduce-scatter.12
  277.3 76.8 reduce-scatter.10
where the time goes:
time: 365 us; the launch traced here: 364 us
  waiting for transfers between devices  180 us (49%)
  blocking collectives  71.3 us (20%)
  matrix products  45.1 us (12%)
  other arithmetic  25.8 us (7%)
  local copies, waits for them, and re-layouts  20.9 us (6%)
  between operations  20 us (5%)
    reduce_scatter x1, waiting for transfers between devices, on_device(): lax.psum_scatter(up_part.astype(jnp.bfloat16), 'dp', scatter_dimension=0,...  76.9 us
    unnamed x6, waiting for transfers between devices  56.6 us
    all_gather x1, waiting for transfers between devices, on_device(): lax.all_gather(normed, 'fsdp', axis=0, tiled=True)  36.6 us
    unnamed x3, blocking collectives  34.8 us
    unnamed x30, local copies, waits for them, and re-layouts  20.4 us
    all_gather x1, blocking collectives, on_device(): lax.all_gather(img_b, 'fsdp', axis=0, tiled=True)  14.2 us
    all_gather x1, blocking collectives, on_device(): group_grad = lax.all_gather(grad_row, 'fsdp', axis=0, tiled=True)  13.3 us
    reduce_scatter x1, waiting for transfers between devices, on_device(): lax.psum_scatter(image_acc.astype(jnp.bfloat16), 'fsdp', scatter_dimensio...  10.2 us
  transfers between devices with their start and end apart: 5, of which 4 were waited for; matrix products, arithmetic and copies ran while one was open for 21% of the time, Pallas kernels for 0%

commit v1 on v0

v1 whole, which is shorter than its diff:
```python
import jax
import jax.numpy as jnp
from jax import lax
from jax.sharding import PartitionSpec as P

KERNEL = 7
SIDE = 8


def unit_rows(matrix):
    values = matrix.astype(jnp.float32)
    length = jnp.sqrt(jnp.sum(values * values, axis=1, keepdims=True) + 1e-06)
    return (values / length, length)


def back_unit(gradient, unit_part, length):
    inner_prod = jnp.sum(unit_part * gradient, axis=1, keepdims=True)
    return (gradient - unit_part * inner_prod) / length


def depthwise(pictures, kernel):
    reach = KERNEL // 2
    padded = jnp.pad(pictures, ((0, 0), (reach, reach), (reach, reach), (0, 0)))
    summed = jnp.zeros_like(pictures)
    for above in range(KERNEL):
        for across in range(KERNEL):
            summed = (
                summed
                + kernel[above * KERNEL + across]
                * padded[:, above : above + SIDE, across : across + SIDE, :]
            )
    return summed


def layer_norm(values, gain_vec, bias_vec):
    centre = jnp.mean(values, axis=-1, keepdims=True)
    centred = values - centre
    inverse = 1.0 / jnp.sqrt(jnp.mean(centred * centred, axis=-1, keepdims=True) + 1e-06)
    normal = centred * inverse
    return (normal * gain_vec + bias_vec, normal, inverse)


def head_back(patch_means, block_mean, image_sum, layer_scale, head_gain, head_bias, w_proj):
    pooled = patch_means.astype(jnp.float32) + layer_scale * block_mean
    head_out, head_norm, inverse = layer_norm(pooled, head_gain, head_bias)
    embed = jnp.dot(head_out.astype(jnp.bfloat16), w_proj, preferred_element_type=jnp.float32)
    embed_unit, embed_len = unit_rows(embed)
    embed_grad = back_unit(image_sum, embed_unit, embed_len).astype(jnp.bfloat16)
    head_grad = jnp.dot(embed_grad, w_proj.T, preferred_element_type=jnp.float32)
    norm_grad = head_grad * head_gain
    pool_grad = inverse * (
        norm_grad
        - jnp.mean(norm_grad, axis=1, keepdims=True)
        - head_norm * jnp.mean(norm_grad * head_norm, axis=1, keepdims=True)
    )
    return (layer_scale * pool_grad / (SIDE * SIDE)).astype(jnp.bfloat16)


def id_columns(ids):
    codes = jnp.stack([ids // 256, ids % 256], axis=1).astype(jnp.bfloat16)
    return jnp.pad(codes, ((0, 0), (0, 126)))


def split_two(values):
    high = lax.reduce_precision(values, 8, 7)
    low = values - high
    return high.astype(jnp.bfloat16), low.astype(jnp.bfloat16)


def pair_tile_coded(images, image_codes, text_rows, text_codes, temper, offset):
    scores = jnp.dot(images, text_rows.T, preferred_element_type=jnp.float32)
    logits = temper * scores + offset
    same = (image_codes[:, 0][:, None] == text_codes[:, 0][None, :]) & (
        image_codes[:, 1][:, None] == text_codes[:, 1][None, :]
    )
    labels = jnp.where(same, 1.0, -1.0)
    weights = (temper * -labels * jax.nn.sigmoid(-labels * logits)).astype(jnp.bfloat16)
    image_part = jnp.dot(weights, text_rows, preferred_element_type=jnp.float32)
    text_part = jnp.dot(weights.T, images, preferred_element_type=jnp.float32)
    return (image_part, text_part)


def on_device(
    img_emb,
    txt_emb,
    img_ids,
    txt_ids,
    temp_log,
    logit_bias,
    block_in,
    dw_kernel,
    ln_gain,
    ln_bias,
    w_up,
    w_down,
    layer_scale,
    head_gain,
    head_bias,
    w_proj,
):
    channels = block_in.shape[1]
    hid_width = w_up.shape[1]
    embed_width = img_emb.shape[1]
    pairs = img_emb.shape[0]
    patches = SIDE * SIDE
    n_dp, n_fsdp = lax.axis_size("dp"), lax.axis_size("fsdp")
    temper = jnp.exp(temp_log[0])
    offset = logit_bias[0]
    img_unit, img_len = unit_rows(img_emb)
    txt_unit, txt_len = unit_rows(txt_emb)
    img_b = jnp.concatenate([img_unit.astype(jnp.bfloat16), id_columns(img_ids)], axis=1)
    txt_b = jnp.concatenate([txt_unit.astype(jnp.bfloat16), id_columns(txt_ids)], axis=1)
    group_img = lax.all_gather(img_b, "fsdp", axis=0, tiled=True)
    column_txt = lax.all_gather(txt_b, "dp", axis=0, tiled=True)
    pictures = block_in.astype(jnp.float32).reshape(1, SIDE, SIDE, channels)
    mixed_rows = depthwise(pictures, dw_kernel).reshape(patches, channels)
    normed = layer_norm(mixed_rows, ln_gain, ln_bias)[0].astype(jnp.bfloat16)
    patch_means = jnp.mean(pictures, axis=(1, 2)).astype(jnp.bfloat16)
    group_normed = lax.all_gather(normed, "fsdp", axis=0, tiled=True)
    image_part, text_part = pair_tile_coded(
        group_img[:, :embed_width],
        group_img[:, embed_width:],
        column_txt[:, :embed_width],
        column_txt[:, embed_width:],
        temper,
        offset,
    )
    hidden = jnp.dot(group_normed, w_up, preferred_element_type=jnp.float32)
    activated, pullback = jax.vjp(jax.nn.gelu, hidden)
    slope = pullback(jnp.ones_like(hidden))[0].astype(jnp.bfloat16)
    active_total = jnp.sum(
        activated.astype(jnp.bfloat16).astype(jnp.float32).reshape(n_fsdp, patches, hid_width),
        axis=1,
    )
    high, low = split_two(active_total / patches)
    both = jnp.dot(jnp.concatenate([high, low]), w_down, preferred_element_type=jnp.float32)
    partial_mean = both[:n_fsdp] + both[n_fsdp:]
    mean_rows = channels // embed_width
    fill = -(pairs + mean_rows) % 16
    terms = jnp.concatenate(
        [
            image_part.astype(jnp.bfloat16).reshape(n_fsdp, pairs, embed_width),
            partial_mean.astype(jnp.bfloat16).reshape(n_fsdp, mean_rows, embed_width),
            jnp.zeros((n_fsdp, fill, embed_width), jnp.bfloat16),
        ],
        axis=1,
    ).reshape(-1, embed_width)
    term_sum = lax.psum_scatter(terms, "fsdp", scatter_dimension=0, tiled=True).astype(jnp.float32)
    image_sum = term_sum[:pairs]
    block_mean = term_sum[pairs : pairs + mean_rows].reshape(1, channels)
    all_slope = lax.all_gather(slope, "dp", axis=0, tiled=True)
    own_normed = lax.all_to_all(group_normed, "dp", split_axis=1, concat_axis=0, tiled=True)
    all_active = lax.all_gather(active_total, "dp", axis=0, tiled=True)
    grad_row = head_back(
        patch_means, block_mean, image_sum[:1], layer_scale, head_gain, head_bias, w_proj
    )
    all_grad = lax.all_gather(grad_row, ("dp", "fsdp"), axis=0, tiled=True)
    row_down = jnp.dot(all_grad, w_down.T, preferred_element_type=jnp.float32)
    hid_grad = (
        (all_slope.reshape(n_dp * n_fsdp, patches, hid_width).astype(jnp.float32) * row_down[:, None, :])
        .astype(jnp.bfloat16)
        .reshape(-1, hid_width)
    )
    w_up_grad = lax.dot_general(
        own_normed, hid_grad, (((0,), (0,)), ((), ())), preferred_element_type=jnp.float32
    )
    share = channels // n_dp
    own_grad = lax.dynamic_slice_in_dim(all_grad, lax.axis_index("dp") * share, share, 1)
    high, low = split_two(all_active)
    w_down_grad = lax.dot_general(
        jnp.concatenate([high, low]),
        jnp.concatenate([own_grad, own_grad]),
        (((0,), (0,)), ((), ())),
        preferred_element_type=jnp.float32,
    )
    text_sum = lax.psum_scatter(
        text_part.astype(jnp.bfloat16), "dp", scatter_dimension=0, tiled=True
    ).astype(jnp.float32)
    img_grad = back_unit(image_sum, img_unit, img_len)
    txt_grad = back_unit(text_sum, txt_unit, txt_len)
    return (img_grad, txt_grad, w_up_grad, w_down_grad)


def solution(mesh):
    in_specs = (
        P(("dp", "fsdp"), None),
        P(("dp", "fsdp"), None),
        P(("dp", "fsdp")),
        P(("dp", "fsdp")),
        P(),
        P(),
        P(("dp", "fsdp"), None),
        P(),
        P(),
        P(),
        P(None, "fsdp"),
        P("fsdp", None),
        P(),
        P(),
        P(),
        P(),
    )
    out_specs = (P(("dp", "fsdp"), None), P(("dp", "fsdp"), None), P("dp", "fsdp"), P("fsdp", "dp"))
    return jax.shard_map(
        on_device, mesh=mesh, in_specs=in_specs, out_specs=out_specs, check_vma=False
    )
```

time: 365 us -> 233 us (0.64)
  waiting for transfers between devices: 180 us -> 19.8 us
  blocking collectives: 71.3 us -> 121 us
  matrix products: 45.1 us -> 33.5 us
  local copies, waits for them, and re-layouts: 20.9 us -> 10.3 us
  starting transfers between devices: 0.2 us -> 3.9 us
    reduce_scatter x2 -> x1, waiting for transfers between devices: 87.2 us -> 0.03 us  [on_device(): lax.psum_scatter(terms, 'fsdp', scatter_dimension=0, tiled=True)]
    all_gather x3 -> x4, blocking collectives: 36.5 us -> 121 us  [the longest x1 69.3 us: on_device(): all_grad = lax.all_gather(grad_row, ('dp', 'fsdp'), axis=0, tiled=True)]
    unnamed x6 -> x4, waiting for transfers between devices: 56.6 us -> 0.07 us
    unnamed x3 -> x0, blocking collectives: 34.8 us -> none
    all_gather x1 -> x2, waiting for transfers between devices: 36.6 us -> 9.81 us  [the longest x1 9.79 us: on_device(): group_normed = lax.all_gather(normed, 'fsdp', axis=0, tiled=True)]
    unnamed x30 -> x32, local copies, waits for them, and re-layouts: 20.4 us -> 0.82 us
    dot_general x7, matrix products: 30.9 us -> 19.2 us  [the longest x1 6.54 us: on_device(): row_down = jnp.dot(all_grad, w_down.T, preferred_element_type=jnp.float32)]
    reduce_scatter x1, waiting for transfers between devices: 0.01 us -> 9.87 us  [on_device(): lax.psum_scatter(text_part.astype(jnp.bfloat16), 'dp', scatter_dimension=...]
  transfers between devices with their start and end apart: 5 -> 5, of which waited for: 4 -> 2; matrix products, arithmetic and copies ran while one was open for 21% -> 19% of each run, Pallas kernels for 0% -> 0%
where the time goes in v1:
time: 233 us; the launch traced here: 232 us
  blocking collectives  121 us (52%)
  matrix products  33.5 us (14%)
  other arithmetic  22.5 us (10%)
  between operations  20.8 us (9%)
  waiting for transfers between devices  19.8 us (8%)
  local copies, waits for them, and re-layouts  10.3 us (4%)
  starting transfers between devices  3.9 us (2%)
    all_gather x1, blocking collectives, on_device(): all_grad = lax.all_gather(grad_row, ('dp', 'fsdp'), axis=0, tiled=True)  69.3 us
    all_gather x1, blocking collectives, on_device(): all_active = lax.all_gather(active_total, 'dp', axis=0, tiled=True)  24.4 us
    all_gather x1, blocking collectives, on_device(): group_img = lax.all_gather(img_b, 'fsdp', axis=0, tiled=True)  17.6 us
    all_gather x1, blocking collectives, on_device(): column_txt = lax.all_gather(txt_b, 'dp', axis=0, tiled=True)  10.1 us
    reduce_scatter x1, waiting for transfers between devices, on_device(): lax.psum_scatter(text_part.astype(jnp.bfloat16), 'dp', scatter_dimension=...  9.87 us
    all_gather x1, waiting for transfers between devices, on_device(): group_normed = lax.all_gather(normed, 'fsdp', axis=0, tiled=True)  9.79 us
    dot_general x1, matrix products, on_device(): row_down = jnp.dot(all_grad, w_down.T, preferred_element_type=jnp.float32)  6.54 us
    reduce_sum x2, other arithmetic, layer_norm(): centre = jnp.mean(values, axis=-1, keepdims=True)  6.11 us
  transfers between devices with their start and end apart: 5, of which 2 were waited for; matrix products, arithmetic and copies ran while one was open for 19% of the time, Pallas kernels for 0%

profile of v1, /device:TPU:0, one launch (start us, length us, event | category | flops | bytes accessed | tf_op | source)
XLA Modules:
  0.0 232.2 jit_solution(10827086138796158804)
XLA Ops:
  8.0 1.5 fusion.163
  9.5 2.1 fusion.161
  11.6 1.9 fusion.162
  13.5 1.1 convert_bitcast_fusion
  14.6 5.5 %fusion.159 = (f32[8,8]{1,0:T(8,128)S(1)}, f32[1,8,8,3072]{3,2,1,0:T(8,128)S(1)}) fusion(f32[3072]{0:T(1024)S(1)} %bitcast.123, f32[3072]{0:T(1024)S(1)} %bitcast.124, f32[3072]{0:T(1024)S(1)} %bitcast.127, f32[3072]{0:T(1024)S(1)} %bitcast.128, f32[3072]{0:T(1024)S(1)} %bitcast.129, f32[3072]{0:T(1024)S(1)} %bitcast.130, f32[3072]{0:T(1024)S(1)} %bitcast.131, ...), kind=kLoop, calls=%fused_computation.268 | loop fusion | flops 19267520 | bytes 2175232 | tf_op jit(solution)/shard_map/reduce_sum | solution.py:36
  20.6 0.9 fusion.115
  23.5 17.6 %all_gather.18 = bf16[128,1152]{1,0:T(8,128)(2,1)S(1)} all-gather(bf16[32,1152]{1,0:T(8,128)(2,1)S(1)} %fusion.131), channel_id=1, replica_groups=mesh['dp'=8,'fsdp'=4] {'fsdp'}, dimensions={0}, use_global_device_ids=true | all-gather | bytes 368640 | tf_op jit(solution)/shard_map/all_gather | solution.py:113
  41.5 10.1 %all_gather.19 = bf16[256,1152]{1,0:T(8,128)(2,1)S(1)} all-gather(bf16[32,1152]{1,0:T(8,128)(2,1)S(1)} %fusion.132), channel_id=1, replica_groups=mesh['dp'=8,'fsdp'=4] {'dp'}, dimensions={0}, use_global_device_ids=true | all-gather | bytes 663552 | tf_op jit(solution)/shard_map/all_gather | solution.py:114
  52.1 1.1 convolution_convert_fusion
  53.6 9.8 %all-gather.5.cloned.1.call-done = bf16[256,3072]{1,0:T(8,128)(2,1)} async-done(((bf16[64,3072]{1,0:T(8,128)(2,1)}), bf16[256,3072]{1,0:T(8,128)(2,1)}) %all-gather.5.cloned.1.call-update) | async-done | bytes 1572880 | tf_op jit(solution)/shard_map/all_gather | solution.py:119
  63.4 6.0 %convert_reduce_fusion = (f32[4,1536]{1,0:T(4,128)S(1)}, f32[256,1536]{1,0:T(8,128)S(1)}) fusion(bf16[256,3072]{1,0:T(8,128)(2,1)} %all-gather.5.cloned.1.call-done, bf16[3072,1536]{1,0:T(8,128)(2,1)} %param.26), kind=kOutput, calls=%fused_computation.59 | convolution fusion | flops 2420238336 | bytes 12607488 | tf_op jit(solution)/shard_map/dot_general | solution.py:128
  70.0 5.0 %fusion.138 = f32[8,3072]{1,0:T(8,128)S(1)} fusion(bf16[1536,3072]{1,0:T(8,128)(2,1)} %param.27, bf16[4,1536]{1,0:T(4,128)(2,1)S(1)} %get-tuple-element.67, bf16[4,1536]{1,0:T(4,128)(2,1)S(1)} %get-tuple-element.66), kind=kOutput, calls=%fused_computation.217 | convolution fusion | flops 75546624 | bytes 9560064 | tf_op jit(solution)/shard_map/dot_general | solution.py:136
  75.1 0.9 maximum_maximum_fusion
  76.0 1.9 fusion.7
  78.0 9.9 %reduce-scatter.5.cloned.1.call-done = bf16[32,1024]{1,0:T(8,128)(2,1)} async-done(((bf16[256,1024]{1,0:T(8,128)(2,1)}), bf16[32,1024]{1,0:T(8,128)(2,1)}) %reduce-scatter.5.cloned.1.call-update) | async-done | bytes 65552 | tf_op jit(solution)/shard_map/reduce_scatter | solution.py:176
  87.9 1.1 fusion.129
  89.0 1.6 fusion.130
  90.6 1.6 copy.43
  92.2 3.7 %all-to-all-start = ((bf16[256,8,384]{0,2,1:T(8,128)(2,1)}), bf16[256,8,384]{0,2,1:T(8,128)(2,1)S(1)}, u32[]{:S(2)}, u32[]{:S(2)}) async-start(bf16[256,8,384]{0,2,1:T(8,128)(2,1)} %bitcast.61), calls=%async_computation.2 | async-start | bytes 3145728 | tf_op jit(solution)/shard_map/all_to_all | solution.py:152
  95.9 24.4 %all-gather.1 = f32[8,4,1536]{2,1,0:T(4,128)S(1)} all-gather(f32[1,4,1536]{2,1,0:T(4,128)S(1)} %bitcast.109), channel_id=1, replica_groups=mesh['dp'=8,'fsdp'=4] {'dp'}, dimensions={0}, use_global_device_ids=true | all-gather | bytes 221184 | tf_op jit(solution)/shard_map/all_gather | solution.py:153
  120.5 0.7 slice.449
  123.9 3.7 %fusion.164 = f32[1,1024]{1,0:T(1,128)S(1)} fusion(bf16[3072,1]{0,1:T(2,128)(2,1)S(1)} %reshape.344, bf16[3072,1024]{1,0:T(8,128)(2,1)} %param.31), kind=kOutput, calls=%fused_computation.272 | convolution fusion | flops 6291456 | bytes 6301696 | tf_op jit(solution)/shard_map/dot_general | solution.py:46
  129.6 0.6 broadcast_multiply_fusion
  130.2 4.5 %fusion.142 = f32[1,3072]{1,0:T(1,128)S(1)} fusion(bf16[3072,1024]{1,0:T(8,128)(2,1)} %param.31, f32[1,1024]{1,0:T(1,128)S(1)} %bitcast.164, f32[48,1024]{1,0:T(8,128)S(1)} %convert_element_type.103, f32[]{:T(128)S(6)} %sqrt.33), kind=kOutput, calls=%fused_computation.228 | convolution fusion | flops 6294528 | bytes 6311940 | tf_op jit(solution)/shard_map/dot_general | solution.py:49
  134.8 0.6 fusion.157
  136.7 69.3 %all-gather = bf16[98304]{0:T(1024)(128)(2,1)S(1)} all-gather(bf16[3072]{0:T(1024)(128)(2,1)S(1)} %multiply_convert_fusion.1), channel_id=2, replica_groups=mesh['dp'=8,'fsdp'=4] {'dp','fsdp'}, dimensions={0}, use_global_device_ids=true | all-gather | bytes 202752 | tf_op jit(solution)/shard_map/all_gather | solution.py:157
  206.4 1.9 fusion.121
  208.3 0.7 subtract_divide_fusion
  209.1 6.5 %fusion.165 = f32[32,1536]{1,0:T(8,128)S(1)} fusion(bf16[32,3072]{1,0:T(8,128)(2,1)S(1)} %reshape.341, bf16[1536,3072]{1,0:T(8,128)(2,1)} %param.27), kind=kOutput, calls=%fused_computation.273 | convolution fusion | flops 301989888 | bytes 9830400 | tf_op jit(solution)/shard_map/dot_general | solution.py:158
  215.6 0.9 copy.44
  216.5 4.0 %fusion = bf16[2048,1536]{1,0:T(8,128)(2,1)S(1)} fusion(bf16[2048,1536]{1,0:T(8,128)(2,1)} %all-gather.7.cloned.1.call-done, f32[32,1536]{1,0:T(8,128)S(1)} %fusion.165), kind=kLoop, calls=%fused_computation.49 | loop fusion | flops 9437184 | bytes 12779520 | tf_op jit(solution)/shard_map/convert_element_type | solution.py:161
  220.5 4.1 %fusion.166 = f32[384,1536]{1,0:T(8,128)} fusion(bf16[2048,384]{1,0:T(8,128)(2,1)S(1)} %bitcast.105, bf16[2048,1536]{1,0:T(8,128)(2,1)S(1)} %fusion), kind=kOutput, calls=%fused_computation.274 | convolution fusion | flops 2415919104 | bytes 10223616 | tf_op jit(solution)/shard_map/dot_general | solution.py:164
  (85 shorter events, 6.1 us)
Async XLA Ops:
  8.0 55.4 %all-gather.5.cloned.1.call-start = ((), (), s32[]{:S(2)}) async-start(), calls=%async_computation.3 | async-start | bytes 1966080 | tf_op jit(solution)/shard_map/all_gather | solution.py:119
  14.6 6.0 %copy-start.10 = (f32[3072]{0:T(1024)S(1)}, f32[3072]{0:T(1024)}, u32[]{:S(2)}) copy-start(f32[3072]{0:T(1024)} %param.25) | copy-start | bytes 36868
  14.6 6.0 %copy-start.11 = (f32[3072]{0:T(1024)S(1)}, f32[3072]{0:T(1024)}, u32[]{:S(2)}) copy-start(f32[3072]{0:T(1024)} %param.24) | copy-start | bytes 36868
  20.1 2.8 %copy-start.2 = (bf16[32,1024]{1,0:T(8,128)(2,1)S(1)}, bf16[32,1024]{1,0:T(8,128)(2,1)}, u32[]{:S(2)}) copy-start(bf16[32,1024]{1,0:T(8,128)(2,1)} %param.16) | copy-start | bytes 196612
  20.1 2.9 %copy-start.13 = (s32[32]{0:T(128)S(1)}, s32[32]{0:T(128)}, u32[]{:S(2)}) copy-start(s32[32]{0:T(128)} %param.18) | copy-start | bytes 388
  20.1 2.9 %copy-start.14 = (s32[32]{0:T(128)S(1)}, s32[32]{0:T(128)}, u32[]{:S(2)}) copy-start(s32[32]{0:T(128)} %param.19) | copy-start | bytes 388
  20.2 21.0 %copy-start.4 = (bf16[32,1024]{1,0:T(8,128)(2,1)S(1)}, bf16[32,1024]{1,0:T(8,128)(2,1)}, u32[]{:S(2)}) copy-start(bf16[32,1024]{1,0:T(8,128)(2,1)} %param.17) | copy-start | bytes 196612
  21.5 66.4 %reduce-scatter.5.cloned.1.call-start = ((), (), s32[]{:S(2)}) async-start(), calls=%async_computation.5 | async-start | bytes 589824 | tf_op jit(solution)/shard_map/reduce_scatter | solution.py:176
  53.2 67.3 %reduce-scatter.3.cloned.1.call-start = ((), (), s32[]{:S(2)}) async-start(), calls=%async_computation.4 | async-start | bytes 491520 | tf_op jit(solution)/shard_map/reduce_scatter | solution.py:148
  69.4 0.6 copy-start.6
  76.0 140.6 %all-gather.7.cloned.1.call-start = ((), (), s32[]{:S(2)}) async-start(), calls=%async_computation.6 | async-start | bytes 7077888 | tf_op jit(solution)/shard_map/all_gather | solution.py:151
  76.0 1.9 copy-start.1
  76.0 14.6 %copy-start = (bf16[256,3072]{1,0:T(8,128)(2,1)S(1)}, bf16[256,3072]{1,0:T(8,128)(2,1)}, u32[]{:S(2)}) copy-start(bf16[256,3072]{1,0:T(8,128)(2,1)} %all-gather.5.cloned.1.call-done) | copy-start | bytes 4718596
  92.2 3.7 %copy-start.7 = (f32[4,1536]{1,0:T(4,128)S(1)}, f32[4,1536]{1,0:T(4,128)}, u32[]{:S(2)}) copy-start(f32[4,1536]{1,0:T(4,128)} %copy-done.6) | copy-start | bytes 73732
  92.2 29.1 %copy-start.9 = (f32[3072]{0:T(1024)S(1)}, f32[3072]{0:T(1024)}, u32[]{:S(2)}) copy-start(f32[3072]{0:T(1024)} %param.28) | copy-start | bytes 36868
  92.2 31.6 %copy-start.8 = (f32[3072]{0:T(1024)S(1)}, f32[3072]{0:T(1024)}, u32[]{:S(2)}) copy-start(f32[3072]{0:T(1024)} %param.29) | copy-start | bytes 36868
  92.2 31.6 %copy-start.12 = (f32[3072]{0:T(1024)S(1)}, f32[3072]{0:T(1024)}, u32[]{:S(2)}) copy-start(f32[3072]{0:T(1024)} %param.30) | copy-start | bytes 36868
  92.2 123.4 %all-to-all-start = ((bf16[256,8,384]{0,2,1:T(8,128)(2,1)}), bf16[256,8,384]{0,2,1:T(8,128)(2,1)S(1)}, u32[]{:S(2)}, u32[]{:S(2)}) async-start(bf16[256,8,384]{0,2,1:T(8,128)(2,1)} %bitcast.61), calls=%async_computation.2 | async-start | bytes 3145728 | tf_op jit(solution)/shard_map/all_to_all | solution.py:152
  123.9 5.1 %copy-start.5 = (bf16[48,1024]{1,0:T(8,128)(2,1)S(1)}, bf16[48,1024]{1,0:T(8,128)(2,1)}, u32[]{:S(2)}) copy-start(bf16[48,1024]{1,0:T(8,128)(2,1)} %reduce-scatter.3.cloned.1.call-done) | copy-start | bytes 294916
  130.2 76.0 %copy-start.3 = (bf16[32,1024]{1,0:T(8,128)(2,1)S(1)}, bf16[32,1024]{1,0:T(8,128)(2,1)}, u32[]{:S(2)}) copy-start(bf16[32,1024]{1,0:T(8,128)(2,1)} %param.16) | copy-start | bytes 196612
Sparse Core Ops, SparseCore 0:
  21.7 41.7 all-gather.4
Sparse Core Ops, SparseCore 1:
  53.3 34.5 reduce-scatter.4
  90.1 20.9 reduce-scatter.2
  112.7 43.7 all-gather.6

commit v2 on v1

--- a/solution.py
+++ b/solution.py
@@ -1,6 +1,10 @@
+import functools
+
 import jax
 import jax.numpy as jnp
 from jax import lax
+from jax.experimental import pallas as pl
+from jax.experimental.pallas import tpu as pltpu
 from jax.sharding import PartitionSpec as P
 
 KERNEL = 7
@@ -40,20 +44,293 @@
     return (normal * gain_vec + bias_vec, normal, inverse)
 
 
-def head_back(patch_means, block_mean, image_sum, layer_scale, head_gain, head_bias, w_proj):
-    pooled = patch_means.astype(jnp.float32) + layer_scale * block_mean
-    head_out, head_norm, inverse = layer_norm(pooled, head_gain, head_bias)
-    embed = jnp.dot(head_out.astype(jnp.bfloat16), w_proj, preferred_element_type=jnp.float32)
-    embed_unit, embed_len = unit_rows(embed)
-    embed_grad = back_unit(image_sum, embed_unit, embed_len).astype(jnp.bfloat16)
-    head_grad = jnp.dot(embed_grad, w_proj.T, preferred_element_type=jnp.float32)
-    norm_grad = head_grad * head_gain
+MESH = pl.DeviceIdType.MESH
+VMEM = pl.BlockSpec(memory_space=pltpu.VMEM)
+ANY = pl.BlockSpec(memory_space=pl.ANY)
+
+
+def greet_peers(n_dp, n_fsdp):
+    d, f = lax.axis_index("dp"), lax.axis_index("fsdp")
+    barrier = pltpu.get_barrier_semaphore()
+    for k in range(1, n_dp):
+        pl.semaphore_signal(barrier, inc=1, device_id={"dp": (d + k) % n_dp}, device_id_type=MESH)
+    for k in range(1, n_fsdp):
+        pl.semaphore_signal(barrier, inc=1, device_id={"fsdp": (f + k) % n_fsdp}, device_id_type=MESH)
+    pl.semaphore_wait(barrier, n_dp + n_fsdp - 2)
+
+
+def push(source, target, send_sem, recv_sem, **peer):
+    return pltpu.make_async_remote_copy(
+        src_ref=source,
+        dst_ref=target,
+        send_sem=send_sem,
+        recv_sem=recv_sem,
+        device_id=peer,
+        device_id_type=MESH,
+    )
+
+
+def first_kernel(n_dp, n_fsdp, spread, norm, img, txt, grp, gimg, ctxt, own, *sems):
+    loc, txt_s, txt_r, img_s, img_r, rgt_s, rgt_r, lft_s, lft_r, col_s, col_r, col_l = sems
+    d, f = lax.axis_index("dp"), lax.axis_index("fsdp")
+    share = norm.shape[1] // n_dp
+    keep = [
+        pltpu.make_async_copy(norm, grp.at[f], loc.at[0]),
+        pltpu.make_async_copy(img, gimg.at[f], loc.at[1]),
+        pltpu.make_async_copy(txt, ctxt.at[d], loc.at[2]),
+    ]
+    for copy in keep:
+        copy.start()
+    greet_peers(n_dp, n_fsdp)
+
+    def right(h, source, b):
+        return push(source, grp.at[b], rgt_s.at[h], rgt_r.at[h], fsdp=f + 1)
+
+    def left(h, source, b):
+        return push(source, grp.at[b], lft_s.at[h], lft_r.at[h], fsdp=f - 1)
+
+    def columns(source, owner):
+        return source.at[:, pl.ds(pl.multiple_of(owner * share, 128), share)]
+
+    def column_copy(k, source, b):
+        peer = (d + k) % n_dp
+        return push(columns(source, peer), own.at[d, b], col_s.at[b, k - 1], col_r.at[b, k - 1], dp=peer)
+
+    def scatter(source, b):
+        if spread:
+            for k in range(1, n_dp):
+                column_copy(k, source, b).start()
+            pltpu.make_async_copy(columns(source, d), own.at[d, b], col_l.at[b]).start()
+
+    @pl.when(f < n_fsdp - 1)
+    def _():
+        right(0, norm, f).start()
+
+    @pl.when(f > 0)
+    def _():
+        left(0, norm, f).start()
+
+    pushes = []
+    for k in range(1, n_fsdp):
+        pushes.append(push(img, gimg.at[f], img_s.at[k - 1], img_r.at[k - 1], fsdp=(f + k) % n_fsdp))
+    for k in range(1, n_dp):
+        pushes.append(push(txt, ctxt.at[d], txt_s.at[k - 1], txt_r.at[k - 1], dp=(d + k) % n_dp))
+    for copy in pushes:
+        copy.start()
+    scatter(norm, f)
+
+    for h in range(1, n_fsdp):
+
+        @pl.when(f - h >= 0)
+        def _():
+            b = f - h
+            right(h - 1, norm, b).wait_recv()
+
+            @pl.when(f < n_fsdp - 1)
+            def _():
+                right(h, grp.at[b], b).start()
+
+            scatter(grp.at[b], b)
+
+        @pl.when(f + h <= n_fsdp - 1)
+        def _():
+            b = f + h
+            left(h - 1, norm, b).wait_recv()
+
+            @pl.when(f > 0)
+            def _():
+                left(h, grp.at[b], b).start()
+
+            scatter(grp.at[b], b)
+
+    for h in range(n_fsdp - 1):
+
+        @pl.when((f - h >= 0) & (f < n_fsdp - 1))
+        def _():
+            right(h, norm, f - h).wait_send()
+
+        @pl.when((f + h <= n_fsdp - 1) & (f > 0))
+        def _():
+            left(h, norm, f + h).wait_send()
+
+    for copy in pushes:
+        copy.wait()
+    for copy in keep:
+        copy.wait()
+    if spread:
+        for b in range(n_fsdp):
+            for k in range(1, n_dp):
+                column_copy(k, norm, b).wait()
+            pltpu.make_async_copy(columns(norm, d), own.at[d, b], col_l.at[b]).wait()
+
+
+def gather_first(n_dp, n_fsdp, normed, img_b, txt_b):
+    rows, channels = normed.shape
+    share = channels // n_dp
+    spread = share % 128 == 0
+    dma = pltpu.SemaphoreType.DMA
+    kind = normed.dtype
+    return pl.pallas_call(
+        functools.partial(first_kernel, n_dp, n_fsdp, spread),
+        out_shape=(
+            jax.ShapeDtypeStruct((n_fsdp, rows, channels), kind),
+            jax.ShapeDtypeStruct((n_fsdp, *img_b.shape), kind),
+            jax.ShapeDtypeStruct((n_dp, *txt_b.shape), kind),
+            jax.ShapeDtypeStruct((n_dp, n_fsdp, rows, share), kind),
+        ),
+        in_specs=[VMEM] * 3,
+        out_specs=(VMEM,) * 4,
+        scratch_shapes=[dma((3,))]
+        + [dma((n_dp - 1,))] * 2
+        + [dma((n_fsdp - 1,))] * 2
+        + [dma((n_fsdp,))] * 4
+        + [dma((n_fsdp, n_dp - 1))] * 2
+        + [dma((n_fsdp,))],
+        compiler_params=pltpu.CompilerParams(
+            collective_id=0, has_side_effects=True, vmem_limit_bytes=40 << 20
+        ),
+    )(normed, img_b, txt_b)
+
+
+def second_kernel(
+    n_dp, n_fsdp, slope, crit, imgs, txts, act, means, scale, gain, bias, proj_hbm,
+    all_slope, all_grad, all_act, img_sum, txt_sum,
+    proj, crit_in, imgs_in, txts_in, lines, *sems,
+):
+    loc, slo_s, slo_r, fwd_s, fwd_r, cri_s, cri_r, ims_s, ims_r, txs_s, txs_r, act_s, act_r, gra_s, gra_r, grd_s, grd_r = sems
+    d, f = lax.axis_index("dp"), lax.axis_index("fsdp")
+    embed_width, channels = proj.shape[1], proj.shape[0]
+    keep = [
+        pltpu.make_async_copy(proj_hbm, proj, loc.at[0]),
+        pltpu.make_async_copy(slope, all_slope.at[d], loc.at[1]),
+        pltpu.make_async_copy(act, all_act.at[d], loc.at[2]),
+    ]
+    for copy in keep:
+        copy.start()
+    greet_peers(n_dp, n_fsdp)
+    critical, late, blocks, passed = [], [], [], []
+    for k in range(1, n_fsdp):
+        peer = (f + k) % n_fsdp
+        critical.append(push(crit.at[peer], crit_in.at[k - 1], cri_s.at[k - 1], cri_r.at[k - 1], fsdp=peer))
+        late.append(push(imgs.at[peer], imgs_in.at[k - 1], ims_s.at[k - 1], ims_r.at[k - 1], fsdp=peer))
+    partner = d + 1 - 2 * (d % 2)
+    for k in range(2, n_dp, 2):
+        blocks.append(push(slope, all_slope.at[d], slo_s.at[k // 2], slo_r.at[k // 2], dp=(d + k) % n_dp))
+        source = (d + n_dp - k) % n_dp
+        passed.append(push(all_slope.at[source], all_slope.at[source], fwd_s.at[k // 2], fwd_r.at[k // 2], dp=partner))
+    near = push(slope, all_slope.at[d], slo_s.at[0], slo_r.at[0], dp=partner)
+    for k in range(1, n_dp):
+        peer = (d + k) % n_dp
+        late.append(push(txts.at[peer], txts_in.at[k - 1], txs_s.at[k - 1], txs_r.at[k - 1], dp=peer))
+        late.append(push(act, all_act.at[d], act_s.at[k - 1], act_r.at[k - 1], dp=peer))
+    for copy in critical + blocks + [near] + late:
+        copy.start()
+
+    for copy in critical:
+        copy.wait()
+    total = crit[f].astype(jnp.float32)
+    for k in range(1, n_fsdp):
+        total = total + crit_in[k - 1].astype(jnp.float32)
+    lines[...] = total
+    image_row = lines[0:1, :]
+    block_mean = jnp.concatenate(
+        [lines[i + 1 : i + 2, :] for i in range(channels // embed_width)], axis=1
+    )
+    pooled = means[...] + scale[...] * block_mean
+    centred = pooled - jnp.mean(pooled, axis=1, keepdims=True)
+    inverse = 1.0 / jnp.sqrt(jnp.mean(centred * centred, axis=1, keepdims=True) + 1e-06)
+    head_norm = centred * inverse
+    head_out = head_norm * gain[...] + bias[...]
+    keep[0].wait()
+    embed = jnp.dot(
+        jnp.broadcast_to(head_out, (16, channels)).astype(jnp.bfloat16),
+        proj[...],
+        preferred_element_type=jnp.float32,
+    )[0:1]
+    embed_len = jnp.sqrt(jnp.sum(embed * embed, axis=1, keepdims=True) + 1e-06)
+    embed_unit = embed / embed_len
+    inner_prod = jnp.sum(embed_unit * image_row, axis=1, keepdims=True)
+    embed_grad = (image_row - embed_unit * inner_prod) / embed_len
+    head_grad = lax.dot_general(
+        jnp.broadcast_to(embed_grad, (16, embed_width)).astype(jnp.bfloat16),
+        proj[...],
+        (((1,), (1,)), ((), ())),
+        preferred_element_type=jnp.float32,
+    )[0:1]
+    norm_grad = head_grad * gain[...]
     pool_grad = inverse * (
         norm_grad
         - jnp.mean(norm_grad, axis=1, keepdims=True)
         - head_norm * jnp.mean(norm_grad * head_norm, axis=1, keepdims=True)
     )
-    return (layer_scale * pool_grad / (SIDE * SIDE)).astype(jnp.bfloat16)
+    row = (scale[...] * pool_grad / (SIDE * SIDE)).astype(jnp.bfloat16).astype(jnp.float32)
+    for i in range(channels // 128):
+        all_grad[d, f, i : i + 1, :] = row[:, i * 128 : (i + 1) * 128]
+    grads = []
+    for k in range(1, n_fsdp):
+        grads.append(push(all_grad.at[d, f], all_grad.at[d, f], gra_s.at[k - 1], gra_r.at[k - 1], fsdp=(f + k) % n_fsdp))
+    for copy in grads:
+        copy.start()
+    for copy in grads:
+        copy.wait()
+    group_grads = []
+    for k in range(1, n_dp):
+        group_grads.append(push(all_grad.at[d], all_grad.at[d], grd_s.at[k - 1], grd_r.at[k - 1], dp=(d + k) % n_dp))
+    for copy in group_grads:
+        copy.start()
+
+    for copy, onward in zip(blocks, passed):
+        copy.wait_recv()
+        onward.start()
+    for copy in late:
+        copy.wait()
+    total = imgs[f].astype(jnp.float32)
+    for k in range(1, n_fsdp):
+        total = total + imgs_in[k - 1].astype(jnp.float32)
+    img_sum[...] = total
+    total = txts[d].astype(jnp.float32)
+    for k in range(1, n_dp):
+        total = total + txts_in[k - 1].astype(jnp.float32)
+    txt_sum[...] = total
+    for copy in blocks:
+        copy.wait_send()
+    for copy in passed + [near] + group_grads + keep[1:]:
+        copy.wait()
+
+
+def exchange_second(n_dp, n_fsdp, slope, crit, imgs, txts, act, means, scale, gain, bias, w_proj):
+    channels, embed_width = w_proj.shape
+    dma = pltpu.SemaphoreType.DMA
+    f32 = jnp.float32
+    pairs = imgs.shape[1]
+    return pl.pallas_call(
+        functools.partial(second_kernel, n_dp, n_fsdp),
+        out_shape=(
+            jax.ShapeDtypeStruct((n_dp, *slope.shape), slope.dtype),
+            jax.ShapeDtypeStruct((n_dp, n_fsdp, channels // 128, 128), f32),
+            jax.ShapeDtypeStruct((n_dp, *act.shape), f32),
+            jax.ShapeDtypeStruct((pairs, embed_width), f32),
+            jax.ShapeDtypeStruct((pairs, embed_width), f32),
+        ),
+        in_specs=[VMEM] * 9 + [ANY],
+        out_specs=(ANY, VMEM, VMEM, VMEM, VMEM),
+        scratch_shapes=[
+            pltpu.VMEM(w_proj.shape, w_proj.dtype),
+            pltpu.VMEM((n_fsdp - 1, *crit.shape[1:]), crit.dtype),
+            pltpu.VMEM((n_fsdp - 1, *imgs.shape[1:]), imgs.dtype),
+            pltpu.VMEM((n_dp - 1, *txts.shape[1:]), txts.dtype),
+            pltpu.VMEM(crit.shape[1:], f32),
+            dma((3,)),
+        ]
+        + [dma((n_dp // 2,))] * 4
+        + [dma((n_fsdp - 1,))] * 4
+        + [dma((n_dp - 1,))] * 4
+        + [dma((n_fsdp - 1,))] * 2
+        + [dma((n_dp - 1,))] * 2,
+        compiler_params=pltpu.CompilerParams(
+            collective_id=1, has_side_effects=True, vmem_limit_bytes=40 << 20
+        ),
+    )(slope, crit, imgs, txts, act, means, scale, gain, bias, w_proj)
 
 
 def id_columns(ids):
@@ -110,13 +387,19 @@
     txt_unit, txt_len = unit_rows(txt_emb)
     img_b = jnp.concatenate([img_unit.astype(jnp.bfloat16), id_columns(img_ids)], axis=1)
     txt_b = jnp.concatenate([txt_unit.astype(jnp.bfloat16), id_columns(txt_ids)], axis=1)
-    group_img = lax.all_gather(img_b, "fsdp", axis=0, tiled=True)
-    column_txt = lax.all_gather(txt_b, "dp", axis=0, tiled=True)
     pictures = block_in.astype(jnp.float32).reshape(1, SIDE, SIDE, channels)
     mixed_rows = depthwise(pictures, dw_kernel).reshape(patches, channels)
     normed = layer_norm(mixed_rows, ln_gain, ln_bias)[0].astype(jnp.bfloat16)
     patch_means = jnp.mean(pictures, axis=(1, 2)).astype(jnp.bfloat16)
-    group_normed = lax.all_gather(normed, "fsdp", axis=0, tiled=True)
+    group_blocks, group_img, column_txt, own_normed = gather_first(n_dp, n_fsdp, normed, img_b, txt_b)
+    group_normed = group_blocks.reshape(-1, channels)
+    group_img = group_img.reshape(n_fsdp * pairs, -1)
+    column_txt = column_txt.reshape(n_dp * pairs, -1)
+    share = channels // n_dp
+    if share % 128 == 0:
+        own_normed = own_normed.reshape(-1, share)
+    else:
+        own_normed = lax.all_to_all(group_normed, "dp", split_axis=1, concat_axis=0, tiled=True)
     image_part, text_part = pair_tile_coded(
         group_img[:, :embed_width],
         group_img[:, embed_width:],
@@ -136,25 +419,31 @@
     both = jnp.dot(jnp.concatenate([high, low]), w_down, preferred_element_type=jnp.float32)
     partial_mean = both[:n_fsdp] + both[n_fsdp:]
     mean_rows = channels // embed_width
-    fill = -(pairs + mean_rows) % 16
-    terms = jnp.concatenate(
+    image_terms = image_part.astype(jnp.bfloat16).reshape(n_fsdp, pairs, embed_width)
+    crit = jnp.concatenate(
         [
-            image_part.astype(jnp.bfloat16).reshape(n_fsdp, pairs, embed_width),
+            image_terms[:, :1],
             partial_mean.astype(jnp.bfloat16).reshape(n_fsdp, mean_rows, embed_width),
-            jnp.zeros((n_fsdp, fill, embed_width), jnp.bfloat16),
+            jnp.zeros((n_fsdp, -(1 + mean_rows) % 16, embed_width), jnp.bfloat16),
         ],
         axis=1,
-    ).reshape(-1, embed_width)
-    term_sum = lax.psum_scatter(terms, "fsdp", scatter_dimension=0, tiled=True).astype(jnp.float32)
-    image_sum = term_sum[:pairs]
-    block_mean = term_sum[pairs : pairs + mean_rows].reshape(1, channels)
-    all_slope = lax.all_gather(slope, "dp", axis=0, tiled=True)
-    own_normed = lax.all_to_all(group_normed, "dp", split_axis=1, concat_axis=0, tiled=True)
-    all_active = lax.all_gather(active_total, "dp", axis=0, tiled=True)
-    grad_row = head_back(
-        patch_means, block_mean, image_sum[:1], layer_scale, head_gain, head_bias, w_proj
-    )
-    all_grad = lax.all_gather(grad_row, ("dp", "fsdp"), axis=0, tiled=True)
+    )
+    all_slope, all_grad, all_active, image_sum, text_sum = exchange_second(
+        n_dp,
+        n_fsdp,
+        slope,
+        crit,
+        image_terms,
+        text_part.astype(jnp.bfloat16).reshape(n_dp, pairs, embed_width),
+        active_total,
+        patch_means.astype(jnp.float32).reshape(1, channels),
+        layer_scale[None],
+        head_gain[None],
+        head_bias[None],
+        w_proj,
+    )
+    all_grad = all_grad.reshape(n_dp * n_fsdp, channels).astype(jnp.bfloat16)
+    all_active = all_active.reshape(n_dp * n_fsdp, hid_width)
     row_down = jnp.dot(all_grad, w_down.T, preferred_element_type=jnp.float32)
     hid_grad = (
         (all_slope.reshape(n_dp * n_fsdp, patches, hid_width).astype(jnp.float32) * row_down[:, None, :])
@@ -164,7 +453,6 @@
     w_up_grad = lax.dot_general(
         own_normed, hid_grad, (((0,), (0,)), ((), ())), preferred_element_type=jnp.float32
     )
-    share = channels // n_dp
     own_grad = lax.dynamic_slice_in_dim(all_grad, lax.axis_index("dp") * share, share, 1)
     high, low = split_two(all_active)
     w_down_grad = lax.dot_general(
@@ -173,9 +461,6 @@
         (((0,), (0,)), ((), ())),
         preferred_element_type=jnp.float32,
     )
-    text_sum = lax.psum_scatter(
-        text_part.astype(jnp.bfloat16), "dp", scatter_dimension=0, tiled=True
-    ).astype(jnp.float32)
     img_grad = back_unit(image_sum, img_unit, img_len)
     txt_grad = back_unit(text_sum, txt_unit, txt_len)
     return (img_grad, txt_grad, w_up_grad, w_down_grad)

time: 233 us -> 138 us (0.59)
  blocking collectives: 121 us -> 0 us
  Pallas kernels: 0 us -> 95.7 us
  waiting for transfers between devices: 19.8 us -> 0 us
  between operations: 20.8 us -> 2.36 us
  matrix products: 33.5 us -> 20.7 us
  other arithmetic: 22.5 us -> 12 us
  starting transfers between devices: 3.9 us -> 0 us
  local copies, waits for them, and re-layouts: 10.3 us -> 6.68 us
    all_gather x4 -> x0, blocking collectives: 121 us -> none  [the longest x1 69.3 us: on_device(): all_grad = lax.all_gather(grad_row, ('dp', 'fsdp'), axis=0, tiled=True)]
    pallas_call x0 -> x2, Pallas kernels: none -> 95.7 us  [the longest x1 50.4 us: exchange_second(): pl.pallas_call(functools.partial(second_kernel, n_dp, n_fsdp), out_shape=...]
    reduce_scatter x2 -> x0, waiting for transfers between devices: 9.89 us -> none  [the longest x1 9.87 us: on_device(): lax.psum_scatter(text_part.astype(jnp.bfloat16), 'dp', scatter_dimension=...]
    all_gather x2 -> x0, waiting for transfers between devices: 9.81 us -> none  [the longest x1 9.79 us: on_device(): group_normed = lax.all_gather(normed, 'fsdp', axis=0, tiled=True)]
    dot_general x2 -> x0, matrix products: 8.28 us -> none  [the longest x1 4.54 us: head_back(): jnp.dot(embed_grad, w_proj.T, preferred_element_type=jnp.float32)]
    all_to_all x1 -> x0, starting transfers between devices: 3.73 us -> none  [on_device(): lax.all_to_all(group_normed, 'dp', split_axis=1, concat_axis=0, tiled=True)]
    dot_general x1, matrix products: 5.01 us -> 1.33 us  [on_device(): jnp.dot(jnp.concatenate([high, low]), w_down, preferred_element_type=jnp....]
    reduce_sum x2 -> x1, other arithmetic: 6.11 us -> 5.51 us  [layer_norm(): centre = jnp.mean(values, axis=-1, keepdims=True)]
  transfers between devices with their start and end apart: 5 -> 0, of which waited for: 2 -> 0; matrix products, arithmetic and copies ran while one was open for 19% -> 0% of each run, Pallas kernels for 0% -> 0%
where the time goes in v2:
time: 138 us; the launch traced here: 137 us
  Pallas kernels  95.7 us (69%)
  matrix products  20.7 us (15%)
  other arithmetic  12 us (9%)
  local copies, waits for them, and re-layouts  6.68 us (5%)
  between operations  2.36 us (2%)
    pallas_call x1, Pallas kernels, exchange_second(): pl.pallas_call(functools.partial(second_kernel, n_dp, n_fsdp), out_shape=...  50.4 us
    pallas_call x1, Pallas kernels, gather_first(): pl.pallas_call(functools.partial(first_kernel, n_dp, n_fsdp, spread), out...  45.2 us
    dot_general x1, matrix products, on_device(): row_down = jnp.dot(all_grad, w_down.T, preferred_element_type=jnp.float32)  6.55 us
    dot_general x1, matrix products, on_device(): hidden = jnp.dot(group_normed, w_up, preferred_element_type=jnp.float32)  5.92 us
    slice x3, local copies, waits for them, and re-layouts, depthwise(): kernel[above * KERNEL + across]  5.59 us
    reduce_sum x1, other arithmetic, layer_norm(): centre = jnp.mean(values, axis=-1, keepdims=True)  5.51 us
    dot_general x1, matrix products, on_device(): lax.dot_general(own_normed, hid_grad, (((0,), (0,)), ((), ())), preferred...  4.08 us

profile of v2, /device:TPU:0, one launch (start us, length us, event | category | flops | bytes accessed | tf_op | source)
XLA Modules:
  0.0 137.4 jit_solution(12186335080666655452)
XLA Ops:
  0.6 1.6 %fusion.154 = (f32[1,3072]{1,0:T(1,128)S(1)}, f32[1,3072]{1,0:T(1,128)S(1)}, f32[1,3072]{1,0:T(1,128)S(1)}, f32[1,3072]{1,0:T(1,128)S(1)}, f32[1,3072]{1,0:T(1,1...) fusion(f32[49,3072]{1,0:T(8,128)} %param.23), kind=kLoop, calls=%fused_computation.251 | loop fusion | bytes 270336 | tf_op jit(solution)/shard_map/slice | solution.py:33
  2.2 2.0 %fusion.152 = (f32[1,3072]{1,0:T(1,128)S(1)}, f32[1,3072]{1,0:T(1,128)S(1)}, f32[1,3072]{1,0:T(1,128)S(1)}, f32[1,3072]{1,0:T(1,128)S(1)}, f32[1,3072]{1,0:T(1,1...) fusion(f32[49,3072]{1,0:T(8,128)} %param.23), kind=kLoop, calls=%fused_computation.249 | loop fusion | bytes 466944 | tf_op jit(solution)/shard_map/slice | solution.py:33
  4.2 2.0 %fusion.153 = (f32[1,3072]{1,0:T(1,128)S(1)}, f32[1,3072]{1,0:T(1,128)S(1)}, f32[1,3072]{1,0:T(1,128)S(1)}, f32[1,3072]{1,0:T(1,128)S(1)}, f32[1,3072]{1,0:T(1,1...) fusion(f32[49,3072]{1,0:T(8,128)} %param.23), kind=kLoop, calls=%fused_computation.250 | loop fusion | bytes 466944 | tf_op jit(solution)/shard_map/slice | solution.py:33
  6.2 1.1 convert_bitcast_fusion
  7.3 5.5 %fusion.150 = (f32[8,8]{1,0:T(8,128)S(1)}, f32[1,8,8,3072]{3,2,1,0:T(8,128)S(1)}) fusion(f32[3072]{0:T(1024)S(1)} %bitcast.137, f32[3072]{0:T(1024)S(1)} %bitcast.138, f32[3072]{0:T(1024)S(1)} %bitcast.140, f32[3072]{0:T(1024)S(1)} %bitcast.141, f32[3072]{0:T(1024)S(1)} %bitcast.142, f32[3072]{0:T(1024)S(1)} %bitcast.143, f32[3072]{0:T(1024)S(1)} %bitcast.144, ...), kind=kLoop, calls=%fused_computation.248 | loop fusion | flops 19267520 | bytes 2175232 | tf_op jit(solution)/shard_map/reduce_sum | solution.py:40
  12.8 0.2 multiply_reduce_fusion
  13.3 0.2 fusion.115.norm
  13.5 0.1 copy.35
  13.6 0.1 fusion.127
  13.8 0.1 fusion.147
  13.9 0.1 copy.36
  14.0 0.1 fusion.128
  14.1 0.1 fusion.148
  14.3 45.2 %shard_map.183 = (bf16[4,64,3072]{2,1,0:T(8,128)(2,1)S(1)}, bf16[4,32,1152]{2,1,0:T(8,128)(2,1)S(1)}, bf16[8,32,1152]{2,1,0:T(8,128)(2,1)S(1)}, bf16[8,4,64,384]{3,2,1,0:T(8,128)(2,1)S(1)}) custom-call(bf16[64,3072]{1,0:T(8,128)(2,1)S(1)} %fusion.115.norm, bf16[32,1152]{1,0:T(8,128)(2,1)S(1)} %get-tuple-element.87.img, ...), custom_call_target="tpu_custom_call" | custom-call | tf_op jit(solution)/shard_map/pallas_call | solution.py:173
  59.5 5.9 %fusion.7 = (bf16[256,1536]{1,0:T(8,128)(2,1)S(1)}, f32[256,1536]{1,0:T(8,128)S(1)}) fusion(bf16[256,3072]{1,0:T(8,128)(2,1)S(1)} %bitcast.120, bf16[3072,1536]{1,0:T(8,128)(2,1)} %param.26), kind=kOutput, calls=%fused_computation.58 | convolution fusion | flops 2422996992 | bytes 13369344 | tf_op jit(solution)/shard_map/dot_general | solution.py:411
  65.4 0.6 convert_reduce_fusion.act
  66.1 1.3 fusion.136
  68.8 0.2 slice_reduce_fusion.1
  69.1 0.1 copy.42
  69.2 0.4 fusion.15
  69.6 0.2 convolution_convert_fusion.1
  70.0 0.1 maximum_maximum_fusion.crit
  70.1 0.3 convolution_convert_fusion
  70.5 50.4 %shard_map.184 = (bf16[8,256,1536]{2,1,0:T(8,128)(2,1)S(1)}, f32[8,4,24,128]{3,2,1,0:T(8,128)S(1)}, f32[8,4,1536]{2,1,0:T(4,128)S(1)}, f32[32,1024]{1,0:T(8,128)S(1)}, f32[32,1024]{1,0:T(8,128)S(1)}) custom-call(bf16[256,1536]{1,0:T(8,128)(2,1)S(1)} %get-tuple-element.85.slope, bf16[4,16,1024]{2,1,0:T(8,128)(2,1)S(1)} %maximum_maximum_fusion.crit, ...), custom_call_target="tpu_custom_call" | custom-call | tf_op jit(solution)/shard_map/pallas_call | solution.py:306
  121.0 0.2 multiply_reduce_fusion.2
  121.2 0.8 subtract_divide_fusion.1
  121.9 0.2 multiply_reduce_fusion.1
  122.1 0.8 subtract_divide_fusion
  122.9 6.6 %fusion.149 = f32[32,1536]{1,0:T(8,128)S(1)} fusion(bf16[1536,3072]{1,0:T(8,128)(2,1)} %param.27, bf16[4,8,24,128]{3,2,1,0:T(8,128)(2,1)S(1)} %bitcast.124), kind=kOutput, calls=%fused_computation.247 | convolution fusion | flops 301989888 | bytes 9830400 | tf_op jit(solution)/shard_map/dot_general | solution.py:447
  129.4 1.8 %fusion = bf16[32,64,1536]{2,1,0:T(8,128)(2,1)S(1)} fusion(bf16[32,64,1536]{2,1,0:T(8,128)(2,1)S(1)} %bitcast.105, f32[32,1536]{1,0:T(8,128)S(1)} %fusion.149), kind=kLoop, calls=%fused_computation.49 | loop fusion | flops 9437184 | bytes 12779520 | tf_op jit(solution)/shard_map/convert_element_type | solution.py:450
  131.2 4.1 %fusion.156 = f32[384,1536]{1,0:T(8,128)} fusion(bf16[2048,384]{1,0:T(8,128)(2,1)S(1)} %bitcast.106, bf16[2048,1536]{1,0:T(8,128)(2,1)S(1)} %bitcast.123), kind=kOutput, calls=%fused_computation.253 | convolution fusion | flops 2415919104 | bytes 10223616 | tf_op jit(solution)/shard_map/dot_general | solution.py:453
  135.5 1.9 %fusion.121 = f32[1536,384]{1,0:T(8,128)} fusion(bf16[32,1536]{1,0:T(8,128)(2,1)S(1)} %get-tuple-element.78, bf16[32,1536]{1,0:T(8,128)(2,1)S(1)} %get-tuple-element.77, bf16[32,384]{1,0:T(8,128)(2,1)S(1)} %constant_dynamic-slice_fusion), kind=kOutput, calls=%fused_computation.184 | convolution fusion | flops 75988992 | bytes 2580480 | tf_op jit(solution)/shard_map/dot_general | solution.py:458
  (53 shorter events, 0.9 us)
Async XLA Ops:
  7.3 6.0 %copy-start.6 = (f32[3072]{0:T(1024)S(1)}, f32[3072]{0:T(1024)}, u32[]{:S(2)}) copy-start(f32[3072]{0:T(1024)} %param.25) | copy-start | bytes 36868
  7.3 6.0 %copy-start.7 = (f32[3072]{0:T(1024)S(1)}, f32[3072]{0:T(1024)}, u32[]{:S(2)}) copy-start(f32[3072]{0:T(1024)} %param.24) | copy-start | bytes 36868
  7.3 6.2 %copy-start.8 = (s32[32]{0:T(128)S(1)}, s32[32]{0:T(128)}, u32[]{:S(2)}) copy-start(s32[32]{0:T(128)} %param.18) | copy-start | bytes 388
  7.3 6.3 %copy-start.4 = (bf16[32,1024]{1,0:T(8,128)(2,1)S(1)}, bf16[32,1024]{1,0:T(8,128)(2,1)}, u32[]{:S(2)}) copy-start(bf16[32,1024]{1,0:T(8,128)(2,1)} %param.16) | copy-start | bytes 196612
  12.8 1.0 copy-start.9
  12.8 1.2 copy-start.5
  59.5 6.5 %slice-start = ((s8[9437184]{0:T(1024)(128)(4,1)}), s8[4194304]{0:T(1024)(128)(4,1)S(1)}, s32[]{:S(2)}) async-start(s8[9437184]{0:T(1024)(128)(4,1)} %bitcast.121), calls=%async_computation | async-start | bytes 8388608
  59.5 6.5 %slice-start.1 = ((s8[9437184]{0:T(1024)(128)(4,1)}), s8[4194304]{0:T(1024)(128)(4,1)S(1)}, s32[]{:S(2)}) async-start(s8[9437184]{0:T(1024)(128)(4,1)} %bitcast.121), calls=%async_computation.1 | async-start | bytes 8388608
  59.5 6.5 %slice-start.2 = ((s8[9437184]{0:T(1024)(128)(4,1)}), s8[1048576]{0:T(1024)(128)(4,1)S(1)}, s32[]{:S(2)}) async-start(s8[9437184]{0:T(1024)(128)(4,1)} %bitcast.121), calls=%async_computation.2 | async-start | bytes 2097152
  69.2 1.2 copy-start.3
  69.6 0.9 copy-start
  69.6 0.9 copy-start.1
  69.6 0.9 copy-start.2

commit v3 on v2

v3 whole, which is shorter than its diff:
```python
import functools

import jax
import jax.numpy as jnp
from jax import lax
from jax.experimental import pallas as pl
from jax.experimental.pallas import tpu as pltpu
from jax.sharding import PartitionSpec as P

KERNEL = 7
SIDE = 8


def unit_rows(matrix):
    values = matrix.astype(jnp.float32)
    length = jnp.sqrt(jnp.sum(values * values, axis=1, keepdims=True) + 1e-06)
    return (values / length, length)


def back_unit(gradient, unit_part, length):
    inner_prod = jnp.sum(unit_part * gradient, axis=1, keepdims=True)
    return (gradient - unit_part * inner_prod) / length


def depthwise(pictures, kernel):
    reach = KERNEL // 2
    padded = jnp.pad(pictures, ((0, 0), (reach, reach), (reach, reach), (0, 0)))
    summed = jnp.zeros_like(pictures)
    for above in range(KERNEL):
        for across in range(KERNEL):
            summed = (
                summed
                + kernel[above * KERNEL + across]
                * padded[:, above : above + SIDE, across : across + SIDE, :]
            )
    return summed


def layer_norm(values, gain_vec, bias_vec):
    centre = jnp.mean(values, axis=-1, keepdims=True)
    centred = values - centre
    inverse = 1.0 / jnp.sqrt(jnp.mean(centred * centred, axis=-1, keepdims=True) + 1e-06)
    normal = centred * inverse
    return (normal * gain_vec + bias_vec, normal, inverse)


MESH = pl.DeviceIdType.MESH
VMEM = pl.BlockSpec(memory_space=pltpu.VMEM)
ANY = pl.BlockSpec(memory_space=pl.ANY)


def greet_peers(n_dp, n_fsdp):
    d, f = lax.axis_index("dp"), lax.axis_index("fsdp")
    barrier = pltpu.get_barrier_semaphore()
    for k in range(1, n_dp):
        pl.semaphore_signal(barrier, inc=1, device_id={"dp": (d + k) % n_dp}, device_id_type=MESH)
    for k in range(1, n_fsdp):
        pl.semaphore_signal(barrier, inc=1, device_id={"fsdp": (f + k) % n_fsdp}, device_id_type=MESH)
    pl.semaphore_wait(barrier, n_dp + n_fsdp - 2)


def push(source, target, send_sem, recv_sem, **peer):
    return pltpu.make_async_remote_copy(
        src_ref=source,
        dst_ref=target,
        send_sem=send_sem,
        recv_sem=recv_sem,
        device_id=peer,
        device_id_type=MESH,
    )


def second_parts(x):
    cubic = 0.044715
    slant = 0.7978845608028654
    square = x * x
    t = jnp.tanh(slant * x * (1.0 + cubic * square))
    half = 0.5 * (1.0 + t)
    slope = half + 0.5 * x * (1.0 - t * t) * slant * (1.0 + 3.0 * cubic * square)
    return x * half, slope


def nt_dot(left, right):
    return lax.dot_general(
        left, right, (((1,), (1,)), ((), ())), preferred_element_type=jnp.float32
    )


def whole_kernel(
    n_dp, n_fsdp, spread, norm, img, txt, temper, offset, means, scale, gain, bias,
    up_hbm, down_hbm, proj_hbm,
    grp, own, all_slope, all_grad, all_act, img_sum, txt_sum,
    up, down, proj, gimg, ctxt, slope, crit, imgs, txts, crit_in, imgs_in, txts_in, lines, partial,
    *sems,
):
    (
        loc, txt_s, txt_r, img_s, img_r, rgt_s, rgt_r, lft_s, lft_r, col_s, col_r, col_l,
        slo_l, slo_s, slo_r, fwd_s, fwd_r, cri_s, cri_r, ims_s, ims_r, txs_s, txs_r,
        act_s, act_r, gra_s, gra_r, grd_s, grd_r,
    ) = sems
    d, f = lax.axis_index("dp"), lax.axis_index("fsdp")
    rows, channels = norm.shape
    share = channels // n_dp
    embed_width = proj.shape[1]
    hid_width = up.shape[1]
    pairs = img.shape[0]
    partner = d + 1 - 2 * (d % 2)
    keep = [
        pltpu.make_async_copy(up_hbm, up, loc.at[0]),
        pltpu.make_async_copy(norm, grp.at[f], loc.at[1]),
        pltpu.make_async_copy(img, gimg.at[f], loc.at[2]),
        pltpu.make_async_copy(txt, ctxt.at[d], loc.at[3]),
        pltpu.make_async_copy(down_hbm, down, loc.at[4]),
        pltpu.make_async_copy(proj_hbm, proj, loc.at[5]),
    ]
    for copy in keep:
        copy.start()
    greet_peers(n_dp, n_fsdp)

    def right(h, source, b):
        return push(source, grp.at[b], rgt_s.at[h], rgt_r.at[h], fsdp=f + 1)

    def left(h, source, b):
        return push(source, grp.at[b], lft_s.at[h], lft_r.at[h], fsdp=f - 1)

    def columns(source, owner):
        return source.at[:, pl.ds(pl.multiple_of(owner * share, 128), share)]

    def column_copy(k, source, b):
        peer = (d + k) % n_dp
        return push(columns(source, peer), own.at[d, b], col_s.at[b, k - 1], col_r.at[b, k - 1], dp=peer)

    def scatter(source, b):
        if spread:
            for k in range(1, n_dp):
                column_copy(k, source, b).start()
            pltpu.make_async_copy(columns(source, d), own.at[d, b], col_l.at[b]).start()

    def slope_copy(k, b):
        peer = partner if k == 0 else (d + k) % n_dp
        return push(slope.at[b], all_slope.at[d, b], slo_s.at[b, k // 2], slo_r.at[b, k // 2], dp=peer)

    def slope_keep(b):
        return pltpu.make_async_copy(slope.at[b], all_slope.at[d, b], slo_l.at[b])

    def onward(k, b):
        spot = all_slope.at[(d + n_dp - k) % n_dp, b]
        return push(spot, spot, fwd_s.at[b, k // 2], fwd_r.at[b, k // 2], dp=partner)

    wide = 256 if hid_width % 256 == 0 else 128

    def expand(source, b):
        def tile(i, carry):
            cols = pl.ds(pl.multiple_of(i * wide, wide), wide)
            hidden = jnp.dot(source[...], up[:, cols], preferred_element_type=jnp.float32)
            active, slant = second_parts(hidden)
            slope[b, :, cols] = slant.astype(jnp.bfloat16)
            active = active.astype(jnp.bfloat16).astype(jnp.float32)
            all_act[d, b, :, cols] = jnp.sum(active, axis=0, keepdims=True)
            return carry

        lax.fori_loop(0, hid_width // wide, tile, 0)
        for k in range(0, n_dp, 2):
            slope_copy(k, b).start()
        slope_keep(b).start()

    @pl.when(f < n_fsdp - 1)
    def _():
        right(0, norm, f).start()

    @pl.when(f > 0)
    def _():
        left(0, norm, f).start()

    img_pushes, txt_pushes = [], []
    for k in range(1, n_fsdp):
        img_pushes.append(push(img, gimg.at[f], img_s.at[k - 1], img_r.at[k - 1], fsdp=(f + k) % n_fsdp))
    for k in range(1, n_dp):
        txt_pushes.append(push(txt, ctxt.at[d], txt_s.at[k - 1], txt_r.at[k - 1], dp=(d + k) % n_dp))
    for copy in img_pushes + txt_pushes:
        copy.start()
    scatter(norm, f)
    keep[0].wait()
    expand(norm, f)

    for copy in keep[2:4] + img_pushes + txt_pushes:
        copy.wait()
    images = gimg[...].reshape(n_fsdp * pairs, -1)
    texts = ctxt[...].reshape(n_dp * pairs, -1)
    image_rows, image_codes = images[:, :embed_width], images[:, embed_width:]
    text_rows, text_codes = texts[:, :embed_width], texts[:, embed_width:]

    def weigh(left_rows, left_codes, right_rows, right_codes):
        logits = temper[...] * nt_dot(left_rows, right_rows) + offset[...]
        labels = jnp.where(nt_dot(left_codes, right_codes) == 0.0, 1.0, -1.0)
        return (temper[...] * -labels * jax.nn.sigmoid(-labels * logits)).astype(jnp.bfloat16)

    weights = weigh(image_rows, image_codes, text_rows, text_codes)
    image_part = jnp.dot(weights, text_rows, preferred_element_type=jnp.float32)
    crit[...] = jnp.zeros_like(crit)
    for p in range(n_fsdp):
        imgs[p] = image_part[p * pairs : (p + 1) * pairs].astype(jnp.bfloat16)
        crit[p, 0:1, :] = image_part[p * pairs : p * pairs + 1]
    weights = weigh(text_rows, text_codes, image_rows, image_codes)
    text_part = jnp.dot(weights, image_rows, preferred_element_type=jnp.float32)
    for p in range(n_dp):
        txts[p] = text_part[p * pairs : (p + 1) * pairs].astype(jnp.bfloat16)

    for h in range(1, n_fsdp):

        @pl.when(f - h >= 0)
        def _():
            b = f - h
            right(h - 1, norm, b).wait_recv()

            @pl.when(f < n_fsdp - 1)
            def _():
                right(h, grp.at[b], b).start()

            scatter(grp.at[b], b)

        @pl.when(f + h <= n_fsdp - 1)
        def _():
            b = f + h
            left(h - 1, norm, b).wait_recv()

            @pl.when(f > 0)
            def _():
                left(h, grp.at[b], b).start()

            scatter(grp.at[b], b)

        @pl.when(f - h >= 0)
        def _():
            expand(grp.at[f - h], f - h)

        @pl.when(f + h <= n_fsdp - 1)
        def _():
            expand(grp.at[f + h], f + h)

    critical, late = [], []
    for k in range(1, n_fsdp):
        peer = (f + k) % n_fsdp
        critical.append(push(crit.at[peer], crit_in.at[k - 1], cri_s.at[k - 1], cri_r.at[k - 1], fsdp=peer))
        late.append(push(imgs.at[peer], imgs_in.at[k - 1], ims_s.at[k - 1], ims_r.at[k - 1], fsdp=peer))
    for k in range(1, n_dp):
        peer = (d + k) % n_dp
        late.append(push(all_act.at[d], all_act.at[d], act_s.at[k - 1], act_r.at[k - 1], dp=peer))
        late.append(push(txts.at[peer], txts_in.at[k - 1], txs_s.at[k - 1], txs_r.at[k - 1], dp=peer))

    totals = jnp.concatenate([all_act[d, b] for b in range(n_fsdp)], axis=0) / (SIDE * SIDE)
    high = totals.astype(jnp.bfloat16)
    low = (totals - high.astype(jnp.float32)).astype(jnp.bfloat16)
    both = jnp.concatenate([high.astype(jnp.float32), low.astype(jnp.float32)], axis=0).astype(jnp.bfloat16)
    keep[4].wait()

    def mean_tile(i, carry):
        cols = pl.ds(pl.multiple_of(i * 256, 256), 256)
        product = jnp.dot(both, down[:, cols], preferred_element_type=jnp.float32)
        partial[:, cols] = product[:n_fsdp] + product[n_fsdp:]
        return carry

    lax.fori_loop(0, channels // 256, mean_tile, 0)
    for p in range(n_fsdp):
        for i in range(channels // embed_width):
            crit[p, i + 1 : i + 2, :] = partial[p : p + 1, i * embed_width : (i + 1) * embed_width]
    for copy in critical + late:
        copy.start()
    for copy in critical:
        copy.wait()
    total = crit[f]
    for k in range(1, n_fsdp):
        total = total + crit_in[k - 1]
    lines[...] = total
    image_row = lines[0:1, :]
    block_mean = jnp.concatenate(
        [lines[i + 1 : i + 2, :] for i in range(channels // embed_width)], axis=1
    )
    pooled = means[...] + scale[...] * block_mean
    centred = pooled - jnp.mean(pooled, axis=1, keepdims=True)
    inverse = 1.0 / jnp.sqrt(jnp.mean(centred * centred, axis=1, keepdims=True) + 1e-06)
    head_norm = centred * inverse
    head_out = head_norm * gain[...] + bias[...]
    keep[5].wait()
    embed = jnp.dot(
        jnp.broadcast_to(head_out, (16, channels)).astype(jnp.bfloat16),
        proj[...],
        preferred_element_type=jnp.float32,
    )[0:1]
    embed_len = jnp.sqrt(jnp.sum(embed * embed, axis=1, keepdims=True) + 1e-06)
    embed_unit = embed / embed_len
    inner_prod = jnp.sum(embed_unit * image_row, axis=1, keepdims=True)
    embed_grad = (image_row - embed_unit * inner_prod) / embed_len
    head_grad = lax.dot_general(
        jnp.broadcast_to(embed_grad, (16, embed_width)).astype(jnp.bfloat16),
        proj[...],
        (((1,), (1,)), ((), ())),
        preferred_element_type=jnp.float32,
    )[0:1]
    norm_grad = head_grad * gain[...]
    pool_grad = inverse * (
        norm_grad
        - jnp.mean(norm_grad, axis=1, keepdims=True)
        - head_norm * jnp.mean(norm_grad * head_norm, axis=1, keepdims=True)
    )
    row = (scale[...] * pool_grad / (SIDE * SIDE)).astype(jnp.bfloat16).astype(jnp.float32)
    for i in range(channels // 128):
        all_grad[d, f, i : i + 1, :] = row[:, i * 128 : (i + 1) * 128]
    grads = []
    for k in range(1, n_fsdp):
        grads.append(push(all_grad.at[d, f], all_grad.at[d, f], gra_s.at[k - 1], gra_r.at[k - 1], fsdp=(f + k) % n_fsdp))
    for copy in grads:
        copy.start()
    for copy in grads:
        copy.wait()
    group_grads = []
    for k in range(1, n_dp):
        group_grads.append(push(all_grad.at[d], all_grad.at[d], grd_s.at[k - 1], grd_r.at[k - 1], dp=(d + k) % n_dp))
    for copy in group_grads:
        copy.start()

    for b in range(n_fsdp):
        for k in range(2, n_dp, 2):
            slope_copy(k, b).wait_recv()
            onward(k, b).start()
    for copy in late:
        copy.wait()
    total = imgs[f].astype(jnp.float32)
    for k in range(1, n_fsdp):
        total = total + imgs_in[k - 1].astype(jnp.float32)
    img_sum[...] = total
    total = txts[d].astype(jnp.float32)
    for k in range(1, n_dp):
        total = total + txts_in[k - 1].astype(jnp.float32)
    txt_sum[...] = total
    keep[1].wait()
    for copy in group_grads:
        copy.wait()
    for h in range(n_fsdp - 1):

        @pl.when((f - h >= 0) & (f < n_fsdp - 1))
        def _():
            right(h, norm, f - h).wait_send()

        @pl.when((f + h <= n_fsdp - 1) & (f > 0))
        def _():
            left(h, norm, f + h).wait_send()

    for b in range(n_fsdp):
        slope_copy(0, b).wait()
        slope_keep(b).wait()
        for k in range(2, n_dp, 2):
            slope_copy(k, b).wait_send()
            onward(k, b).wait()
        if spread:
            for k in range(1, n_dp):
                column_copy(k, norm, b).wait()
            pltpu.make_async_copy(columns(norm, d), own.at[d, b], col_l.at[b]).wait()


def run_whole(n_dp, n_fsdp, normed, img_b, txt_b, temper, offset, means, scale, gain, bias, w_up, w_down, w_proj):
    channels, embed_width = w_proj.shape
    rows = normed.shape[0]
    hid_width = w_up.shape[1]
    pairs = img_b.shape[0]
    share = channels // n_dp
    dma = pltpu.SemaphoreType.DMA
    f32, half = jnp.float32, normed.dtype
    shape = jax.ShapeDtypeStruct
    lines = -(-(1 + channels // embed_width) // 8) * 8
    return pl.pallas_call(
        functools.partial(whole_kernel, n_dp, n_fsdp, share % 128 == 0),
        out_shape=(
            shape((n_fsdp, rows, channels), half),
            shape((n_dp, n_fsdp, rows, share), half),
            shape((n_dp, n_fsdp, rows, hid_width), half),
            shape((n_dp, n_fsdp, channels // 128, 128), f32),
            shape((n_dp, n_fsdp, 1, hid_width), f32),
            shape((pairs, embed_width), f32),
            shape((pairs, embed_width), f32),
        ),
        in_specs=[VMEM] * 9 + [ANY] * 3,
        out_specs=(VMEM, VMEM, ANY, VMEM, VMEM, VMEM, VMEM),
        scratch_shapes=[
            pltpu.VMEM(w_up.shape, half),
            pltpu.VMEM(w_down.shape, half),
            pltpu.VMEM(w_proj.shape, half),
            pltpu.VMEM((n_fsdp, *img_b.shape), half),
            pltpu.VMEM((n_dp, *txt_b.shape), half),
            pltpu.VMEM((n_fsdp, rows, hid_width), half),
            pltpu.VMEM((n_fsdp, lines, embed_width), f32),
            pltpu.VMEM((n_fsdp, pairs, embed_width), half),
            pltpu.VMEM((n_dp, pairs, embed_width), half),
            pltpu.VMEM((n_fsdp - 1, lines, embed_width), f32),
            pltpu.VMEM((n_fsdp - 1, pairs, embed_width), half),
            pltpu.VMEM((n_dp - 1, pairs, embed_width), half),
            pltpu.VMEM((lines, embed_width), f32),
            pltpu.VMEM((n_fsdp, channels), f32),
            dma((6,)),
        ]
        + [dma((n_dp - 1,))] * 2
        + [dma((n_fsdp - 1,))] * 2
        + [dma((n_fsdp,))] * 4
        + [dma((n_fsdp, n_dp - 1))] * 2
        + [dma((n_fsdp,))] * 2
        + [dma((n_fsdp, n_dp // 2))] * 4
        + [dma((n_fsdp - 1,))] * 4
        + [dma((n_dp - 1,))] * 4
        + [dma((n_fsdp - 1,))] * 2
        + [dma((n_dp - 1,))] * 2,
        compiler_params=pltpu.CompilerParams(
            collective_id=0, has_side_effects=True, vmem_limit_bytes=60 << 20
        ),
    )(normed, img_b, txt_b, temper, offset, means, scale, gain, bias, w_up, w_down, w_proj)


def id_columns(ids, sign, flip):
    high, low, one = sign * 256 * (ids // 256), sign * (ids % 256), jnp.ones_like(ids)
    codes = [one, one, high, low] if flip else [high, low, one, one]
    return jnp.pad(jnp.stack(codes, axis=1).astype(jnp.bfloat16), ((0, 0), (0, 124)))


def split_two(values):
    high = lax.reduce_precision(values, 8, 7)
    low = values - high
    return high.astype(jnp.bfloat16), low.astype(jnp.bfloat16)


def on_device(
    img_emb,
    txt_emb,
    img_ids,
    txt_ids,
    temp_log,
    logit_bias,
    block_in,
    dw_kernel,
    ln_gain,
    ln_bias,
    w_up,
    w_down,
    layer_scale,
    head_gain,
    head_bias,
    w_proj,
):
    channels = block_in.shape[1]
    hid_width = w_up.shape[1]
    patches = SIDE * SIDE
    n_dp, n_fsdp = lax.axis_size("dp"), lax.axis_size("fsdp")
    temper = jnp.exp(temp_log[0])
    offset = logit_bias[0]
    img_unit, img_len = unit_rows(img_emb)
    txt_unit, txt_len = unit_rows(txt_emb)
    img_b = jnp.concatenate([img_unit.astype(jnp.bfloat16), id_columns(img_ids, 1, False)], axis=1)
    txt_b = jnp.concatenate([txt_unit.astype(jnp.bfloat16), id_columns(txt_ids, -1, True)], axis=1)
    pictures = block_in.astype(jnp.float32).reshape(1, SIDE, SIDE, channels)
    mixed_rows = depthwise(pictures, dw_kernel).reshape(patches, channels)
    normed = layer_norm(mixed_rows, ln_gain, ln_bias)[0].astype(jnp.bfloat16)
    patch_means = jnp.mean(pictures, axis=(1, 2)).astype(jnp.bfloat16)
    group_blocks, own_normed, all_slope, all_grad, all_active, image_sum, text_sum = run_whole(
        n_dp,
        n_fsdp,
        normed,
        img_b,
        txt_b,
        temper.reshape(1, 1),
        offset.reshape(1, 1),
        patch_means.astype(jnp.float32).reshape(1, channels),
        layer_scale[None],
        head_gain[None],
        head_bias[None],
        w_up,
        w_down,
        w_proj,
    )
    group_normed = group_blocks.reshape(-1, channels)
    share = channels // n_dp
    if share % 128 == 0:
        own_normed = own_normed.reshape(-1, share)
    else:
        own_normed = lax.all_to_all(group_normed, "dp", split_axis=1, concat_axis=0, tiled=True)
    all_grad = all_grad.reshape(n_dp * n_fsdp, channels).astype(jnp.bfloat16)
    all_active = all_active.reshape(n_dp * n_fsdp, hid_width)
    row_down = jnp.dot(all_grad, w_down.T, preferred_element_type=jnp.float32)
    hid_grad = (
        (all_slope.reshape(n_dp * n_fsdp, patches, hid_width).astype(jnp.float32) * row_down[:, None, :])
        .astype(jnp.bfloat16)
        .reshape(-1, hid_width)
    )
    w_up_grad = lax.dot_general(
        own_normed, hid_grad, (((0,), (0,)), ((), ())), preferred_element_type=jnp.float32
    )
    own_grad = lax.dynamic_slice_in_dim(all_grad, lax.axis_index("dp") * share, share, 1)
    high, low = split_two(all_active)
    w_down_grad = lax.dot_general(
        jnp.concatenate([high, low]),
        jnp.concatenate([own_grad, own_grad]),
        (((0,), (0,)), ((), ())),
        preferred_element_type=jnp.float32,
    )
    img_grad = back_unit(image_sum, img_unit, img_len)
    txt_grad = back_unit(text_sum, txt_unit, txt_len)
    return (img_grad, txt_grad, w_up_grad, w_down_grad)


def solution(mesh):
    in_specs = (
        P(("dp", "fsdp"), None),
        P(("dp", "fsdp"), None),
        P(("dp", "fsdp")),
        P(("dp", "fsdp")),
        P(),
        P(),
        P(("dp", "fsdp"), None),
        P(),
        P(),
        P(),
        P(None, "fsdp"),
        P("fsdp", None),
        P(),
        P(),
        P(),
        P(),
    )
    out_specs = (P(("dp", "fsdp"), None), P(("dp", "fsdp"), None), P("dp", "fsdp"), P("fsdp", "dp"))
    return jax.shard_map(
        on_device, mesh=mesh, in_specs=in_specs, out_specs=out_specs, check_vma=False
    )
```

time: 138 us -> 123 us (0.89)
  Pallas kernels: 95.7 us -> 81.1 us
  other arithmetic: 12 us -> 20.2 us
  matrix products: 20.7 us -> 12.7 us
    pallas_call x2 -> x1, Pallas kernels: 95.7 us -> 81.1 us  [run_whole(): pl.pallas_call(functools.partial(whole_kernel, n_dp, n_fsdp, share % 128...]
    dot_general x5 -> x0, matrix products: 8.14 us -> none  [the longest x1 5.92 us: on_device(): hidden = jnp.dot(group_normed, w_up, preferred_element_type=jnp.float32)]
    reduce_sum x2, other arithmetic: 0.39 us -> 2.34 us  [back_unit(): inner_prod = jnp.sum(unit_part * gradient, axis=1, keepdims=True)]
    div x2, other arithmetic: 1.51 us -> 3.38 us  [back_unit(): return (gradient - unit_part * inner_prod) / length]
    convert_element_type x1, other arithmetic: 0.2 us -> 1.67 us  [on_device(): normed = layer_norm(mixed_rows, ln_gain, ln_bias)[0].astype(jnp.bfloat16)]
where the time goes in v3:
time: 123 us; the launch traced here: 122 us
  Pallas kernels  81.1 us (66%)
  other arithmetic  20.2 us (16%)
  matrix products  12.7 us (10%)
  local copies, waits for them, and re-layouts  6.01 us (5%)
  between operations  2.2 us (2%)
    pallas_call x1, Pallas kernels, run_whole(): pl.pallas_call(functools.partial(whole_kernel, n_dp, n_fsdp, share % 128...  81.1 us
    dot_general x1, matrix products, on_device(): row_down = jnp.dot(all_grad, w_down.T, preferred_element_type=jnp.float32)  6.7 us
    reduce_sum x1, other arithmetic, layer_norm(): centre = jnp.mean(values, axis=-1, keepdims=True)  5.51 us
    slice x3, local copies, waits for them, and re-layouts, depthwise(): kernel[above * KERNEL + across]  5.49 us
    dot_general x1, matrix products, on_device(): lax.dot_general(own_normed, hid_grad, (((0,), (0,)), ((), ())), preferred...  4.05 us
    div x2, other arithmetic, back_unit(): return (gradient - unit_part * inner_prod) / length  3.38 us

profile of v3, /device:TPU:0, one launch (start us, length us, event | category | flops | bytes accessed | tf_op | source)
XLA Modules:
  0.0 122.2 jit_solution(13910240619653267204)
XLA Ops:
  0.7 1.5 %fusion.129 = (f32[1,3072]{1,0:T(1,128)S(1)}, f32[1,3072]{1,0:T(1,128)S(1)}, f32[1,3072]{1,0:T(1,128)S(1)}, f32[1,3072]{1,0:T(1,128)S(1)}, f32[1,3072]{1,0:T(1,1...) fusion(f32[49,3072]{1,0:T(8,128)} %param.23), kind=kLoop, calls=%fused_computation.213 | loop fusion | bytes 270336 | tf_op jit(solution)/shard_map/slice | solution.py:33
  2.2 2.1 %fusion.127 = (f32[1,3072]{1,0:T(1,128)S(1)}, f32[1,3072]{1,0:T(1,128)S(1)}, f32[1,3072]{1,0:T(1,128)S(1)}, f32[1,3072]{1,0:T(1,128)S(1)}, f32[1,3072]{1,0:T(1,1...) fusion(f32[49,3072]{1,0:T(8,128)} %param.23), kind=kLoop, calls=%fused_computation.211 | loop fusion | bytes 466944 | tf_op jit(solution)/shard_map/slice | solution.py:33
  4.3 1.9 %fusion.128 = (f32[1,3072]{1,0:T(1,128)S(1)}, f32[1,3072]{1,0:T(1,128)S(1)}, f32[1,3072]{1,0:T(1,128)S(1)}, f32[1,3072]{1,0:T(1,128)S(1)}, f32[1,3072]{1,0:T(1,1...) fusion(f32[49,3072]{1,0:T(8,128)} %param.23), kind=kLoop, calls=%fused_computation.212 | loop fusion | bytes 466944 | tf_op jit(solution)/shard_map/slice | solution.py:33
  6.2 1.1 convert_bitcast_fusion
  7.2 5.5 %fusion.125 = (f32[8,8]{1,0:T(8,128)S(1)}, f32[1,8,8,3072]{3,2,1,0:T(8,128)S(1)}) fusion(f32[3072]{0:T(1024)S(1)} %bitcast.106, f32[3072]{0:T(1024)S(1)} %bitcast.107, f32[3072]{0:T(1024)S(1)} %bitcast.110, f32[3072]{0:T(1024)S(1)} %bitcast.111, f32[3072]{0:T(1024)S(1)} %bitcast.112, f32[3072]{0:T(1024)S(1)} %bitcast.113, f32[3072]{0:T(1024)S(1)} %bitcast.114, ...), kind=kLoop, calls=%fused_computation.210 | loop fusion | flops 19267520 | bytes 2175232 | tf_op jit(solution)/shard_map/reduce_sum | solution.py:40
  12.7 0.2 multiply_reduce_fusion
  13.0 0.1 sqrt.22
  13.1 0.1 div.65
  13.2 1.7 %fusion.100.norm = bf16[64,3072]{1,0:T(8,128)(2,1)} fusion(f32[1,8,8,3072]{3,2,1,0:T(8,128)S(1)} %get-tuple-element.17, f32[3072]{0:T(1024)} %param.25, f32[3072]{0:T(1024)} %param.24, f32[64]{0:T(128)S(1)} %sqrt.22, f32[64]{0:T(128)S(1)} %div.65), kind=kLoop, calls=%fused_computation.152 | loop fusion | flops 983040 | bytes 1204736 | tf_op jit(solution)/shard_map/convert_element_type | solution.py:459
  14.9 0.1 copy.24
  15.0 0.1 fusion.108
  15.1 0.1 fusion.122
  15.2 0.6 fusion.110.img
  15.9 0.1 copy.25
  16.0 0.1 fusion.109
  16.1 0.1 fusion.123
  16.2 0.6 fusion.111.txt
  18.2 0.1 convert_reduce_fusion
  18.3 0.6 fusion.115
  18.9 81.1 %shard_map.183 = (bf16[4,64,3072]{2,1,0:T(8,128)(2,1)}, bf16[8,4,64,384]{3,2,1,0:T(8,128)(2,1)}, bf16[8,4,64,1536]{3,2,1,0:T(8,128)(2,1)}, f32[8,4,24,128]{3,2,1...) custom-call(bf16[64,3072]{1,0:T(8,128)(2,1)} %fusion.100.norm, ...), custom_call_target="tpu_custom_call" | custom-call | tf_op jit(solution)/shard_map/pallas_call | solution.py:371
  100.0 1.2 %multiply_reduce_fusion.2 = f32[32]{0:T(128)S(1)} fusion(f32[32,1024]{1,0:T(8,128)} %get-tuple-element.10, f32[32]{0:T(128)S(1)} %add_sqrt_fusion.1, bf16[32,1024]{1,0:T(8,128)(2,1)S(1)} %copy-done.2), kind=kLoop, calls=%fused_computation.174 | loop fusion | flops 131040 | bytes 196864 | tf_op jit(solution)/shard_map/reduce_sum | solution.py:21
  101.2 1.7 %subtract_divide_fusion.1 = f32[32,1024]{1,0:T(8,128)} fusion(f32[32,1024]{1,0:T(8,128)} %get-tuple-element.10, f32[32]{0:T(128)S(1)} %multiply_reduce_fusion.2, f32[32]{0:T(128)S(1)} %add_sqrt_fusion.1, bf16[32,1024]{1,0:T(8,128)(2,1)S(1)} %copy-done.2), kind=kLoop, calls=%fused_computation.173 | loop fusion | flops 163840 | bytes 327936 | tf_op jit(solution)/shard_map/div | solution.py:22
  102.9 1.1 multiply_reduce_fusion.1
  104.0 1.7 %subtract_divide_fusion = f32[32,1024]{1,0:T(8,128)} fusion(f32[32,1024]{1,0:T(8,128)} %get-tuple-element.11, f32[32]{0:T(128)S(1)} %multiply_reduce_fusion.1, f32[32]{0:T(128)S(1)} %add_sqrt_fusion, bf16[32,1024]{1,0:T(8,128)(2,1)S(1)} %copy-done.3), kind=kLoop, calls=%fused_computation.171 | loop fusion | flops 163840 | bytes 327936 | tf_op jit(solution)/shard_map/div | solution.py:22
  105.7 1.0 convert_element_type.92
  106.7 6.7 %fusion.124 = f32[32,1536]{1,0:T(8,128)S(1)} fusion(bf16[1536,3072]{1,0:T(8,128)(2,1)} %down_hbm.1, bf16[4,8,24,128]{3,2,1,0:T(8,128)(2,1)S(1)} %bitcast.94), kind=kOutput, calls=%fused_computation.209 | convolution fusion | flops 301989888 | bytes 9830400 | tf_op jit(solution)/shard_map/dot_general | solution.py:485
  113.4 0.0 slice-done
  113.5 2.0 %fusion = bf16[32,64,1536]{2,1,0:T(8,128)(2,1)S(1)} fusion(bf16[8,4,64,1536]{3,2,1,0:T(8,128)(2,1)S(1)} %bitcast.92, f32[32,1536]{1,0:T(8,128)S(1)} %fusion.124), kind=kLoop, calls=%fused_computation.49 | loop fusion | flops 9437184 | bytes 12779520 | tf_op jit(solution)/shard_map/convert_element_type | solution.py:488
  115.5 4.0 %fusion.130 = f32[384,1536]{1,0:T(8,128)} fusion(bf16[2048,384]{1,0:T(8,128)(2,1)S(1)} %bitcast.93, bf16[2048,1536]{1,0:T(8,128)(2,1)S(1)} %bitcast.90), kind=kOutput, calls=%fused_computation.214 | convolution fusion | flops 2415919104 | bytes 10223616 | tf_op jit(solution)/shard_map/dot_general | solution.py:491
  119.6 0.5 reduce.4
  120.1 0.1 reshape.284
  120.3 1.9 %fusion.102 = f32[1536,384]{1,0:T(8,128)} fusion(bf16[32,1536]{1,0:T(8,128)(2,1)S(1)} %get-tuple-element.68, bf16[32,1536]{1,0:T(8,128)(2,1)S(1)} %get-tuple-element.67, bf16[32,384]{1,0:T(8,128)(2,1)S(1)} %constant_dynamic-slice_fusion), kind=kOutput, calls=%fused_computation.158 | convolution fusion | flops 75988992 | bytes 2580480 | tf_op jit(solution)/shard_map/dot_general | solution.py:496
  (28 shorter events, 0.2 us)
Async XLA Ops:
  0.6 17.5 %copy-start.1 = (bf16[64,3072]{1,0:T(8,128)(2,1)S(1)}, bf16[64,3072]{1,0:T(8,128)(2,1)}, u32[]{:S(2)}) copy-start(bf16[64,3072]{1,0:T(8,128)(2,1)} %param.22) | copy-start | bytes 1179652
  0.6 14.2 %copy-start.5 = (s32[32]{0:T(128)S(1)}, s32[32]{0:T(128)}, u32[]{:S(2)}) copy-start(s32[32]{0:T(128)} %param.19) | copy-start | bytes 388
  0.7 14.2 %copy-start.6 = (s32[32]{0:T(128)S(1)}, s32[32]{0:T(128)}, u32[]{:S(2)}) copy-start(s32[32]{0:T(128)} %param.18) | copy-start | bytes 388
  0.7 14.3 %copy-start.2 = (bf16[32,1024]{1,0:T(8,128)(2,1)S(1)}, bf16[32,1024]{1,0:T(8,128)(2,1)}, u32[]{:S(2)}) copy-start(bf16[32,1024]{1,0:T(8,128)(2,1)} %param.16) | copy-start | bytes 196612
  0.7 15.3 %copy-start.3 = (bf16[32,1024]{1,0:T(8,128)(2,1)S(1)}, bf16[32,1024]{1,0:T(8,128)(2,1)}, u32[]{:S(2)}) copy-start(bf16[32,1024]{1,0:T(8,128)(2,1)} %param.17) | copy-start | bytes 196612
  100.0 13.5 %slice-start = ((s8[6291456]{0:T(1024)(128)(4,1)}), s8[4194304]{0:T(1024)(128)(4,1)S(1)}, s32[]{:S(2)}) async-start(s8[6291456]{0:T(1024)(128)(4,1)} %bitcast.91), calls=%async_computation | async-start | bytes 8388608
  106.7 6.7 %slice-start.1 = ((s8[6291456]{0:T(1024)(128)(4,1)}), s8[2097152]{0:T(1024)(128)(4,1)S(1)}, s32[]{:S(2)}) async-start(s8[6291456]{0:T(1024)(128)(4,1)} %bitcast.91), calls=%async_computation.1 | async-start | bytes 4194304
  113.5 2.0 %copy-start = (bf16[8,4,64,384]{3,2,1,0:T(8,128)(2,1)S(1)}, bf16[8,4,64,384]{3,2,1,0:T(8,128)(2,1)}, u32[]{:S(2)}) copy-start(bf16[8,4,64,384]{3,2,1,0:T(8,128)(2,1)} %get-tuple-element.12) | copy-start | bytes 4718596
  115.5 4.1 %copy-start.4 = (f32[8,4,1,1536]{3,2,1,0:T(1,128)S(1)}, f32[8,4,1,1536]{3,2,1,0:T(1,128)}, u32[]{:S(2)}) copy-start(f32[8,4,1,1536]{3,2,1,0:T(1,128)} %get-tuple-element.15) | copy-start | bytes 589828
